TPU v7x, 512 devices: a whole 4x4x16 slice. The times are simulated.
512 devices in a mesh: fit: 8 (over y, z_hi), ao: 64 (over z_lo, x, core).
Axes of the slice: x: 4, y: 4, z: 16 (z_hi: 2, z_lo: 8; z = z_hi * 8 + z_lo), core: 2. Of those that a mesh axis runs over, the one named last changes fastest.
Arguments:
- occ_blocks: bfloat16 [98304, 512], P(('fit', 'ao')), may hold values from -6 to 6
- resident: bfloat16 [131072, 4096], P(('fit', 'ao')), may hold values from -0.046875 to 0.046875
- row_tiles: int32 [512, 8, 96], P(('fit', 'ao')), may hold values from 0 to 95, as said below
- row_pairs: int32 [3, 512, 8, 96], P(None, ('fit', 'ao')), may hold values from -1 to 31, as said below
- live_rows: int32 [512, 8], P(('fit', 'ao')), may hold values from 1 to 96, as said below
- tile_list: int32 [64, 96], replicated, may hold values from 0 to 1023, as said below
- owner_slot: int32 [256], replicated, may hold values from 0 to 511, as said below
Outputs:
- half_exchange: bfloat16 [512, 64, 512], P('ao', 'fit')
Inputs may be any that keep to these rules, and one draw needn't show every extreme that they name: `row_tiles`: within each group and cycle step the 96 entries are a permutation of 0 to 95. `row_pairs`: each entry is a resident tile index, or -1 where the row has no tile for that fitting block; rows at or beyond live_rows are -1. Within a group and cycle step, live rows whose tiles share an AO block name the same resident tile for the same fitting block. `live_rows`: in every draw some group has all 96 rows live at some cycle step. `tile_list`: codes within a column are distinct and name AO blocks that some owner holds. A column names at most 2 tiles whose AO blocks belong to one owner device (owner_slot // 8); in every draw some owner gets exactly 2 from every column. AO blocks take distinct slots; the owner device of block b is owner_slot[b] // 8; an owner holds 0 to 8 blocks in its first slots, and some owner holds exactly 8.
All inputs are finite; a program needn't handle non-finite values.
Results may differ from a plain program's by a relative error of at most 0.001.
Values may be sent and summed in bfloat16 or wider, within the bound.
A program may use at most 64 MiB of HBM per device.

v0:
```python
import jax
import jax.numpy as jnp
from jax import lax
from jax.sharding import PartitionSpec as P

AB = 64
FB = 64
OB = 128
OWN_CAP = 8
CAP = 2


def from_behind(block, axis, distance):
    devices = range(lax.axis_size(axis))
    route = [((i - distance) % len(devices), i) for i in devices]
    return lax.ppermute(block, axis, route)


def contract(
    partial_value, upiece, cycle_step, resident, row_tiles, row_pairs, live_rows, tile_occ
):
    fit_count = live_rows.shape[1]
    pair_step = resident.shape[0] // fit_count
    row_width = row_tiles.shape[2]
    block_rows = row_width // 3
    fit_blocks = row_pairs.shape[0]
    occ_count = upiece.shape[1] // OB
    grouped = upiece.reshape(fit_blocks, FB, occ_count, OB)
    step_tiles = lax.dynamic_index_in_dim(row_tiles[0], cycle_step, 0, keepdims=False)
    step_pairs = lax.dynamic_index_in_dim(row_pairs[:, 0], cycle_step, 1, keepdims=False)
    live_count = lax.dynamic_index_in_dim(live_rows[0], cycle_step, 0, keepdims=False)

    def one_block(block_num, running):
        offset = block_num * block_rows
        tile_ids = lax.dynamic_slice_in_dim(step_tiles, offset, block_rows)
        pair_ids = lax.dynamic_slice_in_dim(step_pairs, offset, block_rows, axis=1)
        in_range = offset + jnp.arange(block_rows) < live_count
        usable = (pair_ids >= 0) & in_range[None, :]
        picked = resident[cycle_step * pair_step + jnp.maximum(pair_ids, 0)]
        picked = jnp.where(usable[:, :, None], picked, jnp.zeros((), picked.dtype))
        picked = picked.reshape(fit_blocks, block_rows, AB, FB)
        chosen = grouped[:, :, tile_occ[tile_ids], :]
        product = jnp.einsum("jrmp,jprc->rmc", picked, chosen, preferred_element_type=jnp.float32)
        return running.at[tile_ids].add(product)

    block_total = (live_count + block_rows - 1) // block_rows
    return lax.fori_loop(0, block_total, one_block, partial_value)


def routing(tile_list, owner_slot, occ_count):
    row_width = tile_list.shape[1]
    slot_ids = owner_slot[tile_list // occ_count]
    owners = slot_ids // OWN_CAP
    same_owner = owners[:, :, None] == owners[:, None, :]
    earlier = jnp.arange(row_width)[None, :] < jnp.arange(row_width)[:, None]
    owner_ranks = jnp.sum((same_owner & earlier[None, :, :]).astype(jnp.int32), axis=2)
    targets = slot_ids % OWN_CAP * occ_count + tile_list % occ_count
    return (owners, owner_ranks, targets)


def pack_tiles(tiles_here, owners_row, ranks_row, ao_count):
    buffer = jnp.zeros((ao_count * CAP,) + tiles_here.shape[1:], tiles_here.dtype)
    buffer = buffer.at[owners_row * CAP + ranks_row].set(tiles_here)
    return buffer.reshape((ao_count, CAP) + tiles_here.shape[1:])


def unpack(received, owners, owner_ranks, targets, column, occ_count):
    ao_count = owners.shape[0]
    received = received.reshape((ao_count * CAP,) + received.shape[2:])
    position = jnp.arange(ao_count)[:, None] * CAP + owner_ranks
    position = jnp.where(owners == column, position, ao_count * CAP)
    target_at = jnp.full((ao_count * CAP,), OWN_CAP * occ_count, jnp.int32)
    target_at = target_at.at[position.reshape(-1)].set(targets.reshape(-1), mode="drop")
    summed = jnp.zeros((OWN_CAP * occ_count,) + received.shape[1:], jnp.float32)
    summed = summed.at[target_at].add(received, mode="drop")
    height = received.shape[1]
    return (
        summed.reshape(OWN_CAP, occ_count, height, OB)
        .transpose(0, 2, 1, 3)
        .reshape(OWN_CAP, height, occ_count * OB)
    )


def shards(occ_blocks, resident, row_tiles, row_pairs, live_rows, tile_list, owner_slot):
    fit_count = lax.axis_size("fit")
    ao_count = lax.axis_size("ao")
    column = lax.axis_index("ao")
    occ_count = occ_blocks.shape[1] // OB
    tile_codes = lax.dynamic_index_in_dim(tile_list, column, 0, keepdims=False)
    tile_occ = tile_codes % occ_count
    row_width = tile_list.shape[1]
    partial_value = jnp.zeros((row_width, AB, OB), jnp.float32)

    def advance(running, upiece, cycle_step):
        return contract(
            running, upiece, cycle_step, resident, row_tiles, row_pairs, live_rows, tile_occ
        )

    partial_value = advance(partial_value, occ_blocks, 0)

    def cycle_turn(cycle_step, cycle_state):
        upiece, running = cycle_state
        upiece = from_behind(upiece, "fit", 1)
        return (upiece, advance(running, upiece, cycle_step))

    _, partial_value = lax.fori_loop(1, fit_count, cycle_turn, (occ_blocks, partial_value))
    owners, owner_ranks, targets = routing(tile_list, owner_slot, occ_count)
    owners_row = lax.dynamic_index_in_dim(owners, column, 0, keepdims=False)
    ranks_row = lax.dynamic_index_in_dim(owner_ranks, column, 0, keepdims=False)
    outgoing = pack_tiles(partial_value, owners_row, ranks_row, ao_count)
    received = lax.all_to_all(outgoing, "ao", split_axis=0, concat_axis=0, tiled=True)
    summed = unpack(received, owners, owner_ranks, targets, column, occ_count)
    result = lax.psum_scatter(summed, "fit", scatter_dimension=1, tiled=True)
    return result.astype(jnp.bfloat16)


def solution(mesh):
    return jax.shard_map(
        shards,
        mesh=mesh,
        in_specs=(
            P(("fit", "ao"), None),
            P(("fit", "ao"), None),
            P(("fit", "ao"), None, None),
            P(None, ("fit", "ao"), None, None),
            P(("fit", "ao"), None),
            P(),
            P(),
        ),
        out_specs=P("ao", "fit", None),
        check_vma=False,
    )
```

profile of v0, /device:TPU:1, one launch (start us, length us, event | category | flops | bytes accessed | tf_op | source)
XLA Modules:
  0.0 931.9 jit_solution(14406453685444881592)
XLA Ops:
  14.6 15.0 %while.62 = (s32[]{:T(128)}, f32[96,64,128]{2,1,0:T(8,128)}, s32[]{:T(128)}, s32[96]{0:T(128)S(1)}, s32[3,96]{1,0:T(4,128)S(1)}, /*index=5*/s32[]{:T(128)}, bf16...) while((s32[]{:T(128)}, f32[96,64,128]{2,1,0:T(8,128)}, ...), condition=%wide.region_4.5_spmd, body=%wide.region_2.4_spmd.sunk | while | flops 101322280 | bytes 12862079 | solution.py:47
  29.7 38.5 %gather_fusion.6 = s32[6144]{0:T(1024)S(1)} fusion(s32[256]{0:T(256)S(1)} %copy-done, s32[6144]{0:T(1024)S(1)} %broadcast_clamp_fusion), kind=kCustom, calls=%fused_computation.6 | custom fusion | bytes 73728 | tf_op jit(solution)/shard_map/gather | solution.py:52
  72.0 459.4 %while.64 = (s32[]{:T(128)}, bf16[192,512]{1,0:T(8,128)(2,1)S(1)}, f32[96,64,128]{2,1,0:T(8,128)}, s32[1,8]{1,0:T(1,128)}, s32[1,8,96]{2,1,0:T(8,128)}, /*index=...) while((s32[]{:T(128)}, bf16[192,512]{1,0:T(8,128)(2,1)S(1)}, ...), condition=%wide.region_9.10_spmd, body=%wide.region_5.9_spmd.sunk | while | flops 101322688 | bytes 14832352 | solution.py:106
  72.0 46.2 %collective-permute-start = (bf16[192,512]{1,0:T(8,128)(2,1)S(1)}, bf16[192,512]{1,0:T(8,128)(2,1)S(1)}, u32[]{:S(2)}, u32[]{:S(2)}) collective-permute-start(bf16[192,512]{1,0:T(8,128)(2,1)S(1)} %get-tuple-element.944), channel_id=1, source_target_pairs={{448,0},{0,64},{64,128},{128,192},{192,256},{256,320},{320,384},{3... | collective-permute-start | bytes 589832 | tf_op jit(solution)/shard_map/while/body/eval_jaxpr/ppermute | solution.py:16
  122.0 5.9 collective-permute-done
  127.9 15.7 %while.65 = (s32[]{:T(128)}, f32[96,64,128]{2,1,0:T(8,128)}, s32[]{:T(128)}, s32[96]{0:T(128)}, s32[3,96]{1,0:T(4,128)S(1)}, /*index=5*/s32[]{:T(128)}, s32[]{:T...) while((s32[]{:T(128)}, f32[96,64,128]{2,1,0:T(8,128)}, ...), condition=%wide.region_8.8_spmd, body=%wide.region_6.7_spmd.sunk | while | flops 101322664 | bytes 12862631 | solution.py:47
  143.7 22.5 %collective-permute-start = (bf16[192,512]{1,0:T(8,128)(2,1)S(1)}, bf16[192,512]{1,0:T(8,128)(2,1)S(1)}, u32[]{:S(2)}, u32[]{:S(2)}) collective-permute-start(bf16[192,512]{1,0:T(8,128)(2,1)S(1)} %get-tuple-element.944), channel_id=1, source_target_pairs={{448,0},{0,64},{64,128},{128,192},{192,256},{256,320},{320,384},{3... | collective-permute-start | bytes 589832 | tf_op jit(solution)/shard_map/while/body/eval_jaxpr/ppermute | solution.py:16
  169.9 19.6 %collective-permute-done = bf16[192,512]{1,0:T(8,128)(2,1)S(1)} collective-permute-done((bf16[192,512]{1,0:T(8,128)(2,1)S(1)}, bf16[192,512]{1,0:T(8,128)(2,1)S(1)}, u32[]{:S(2)}, u32[]{:S(2)}) %collective-permute-start) | collective-permute-done | bytes 196640 | tf_op jit(solution)/shard_map/while/body/eval_jaxpr/ppermute | solution.py:16
  189.6 15.7 %while.65 = (s32[]{:T(128)}, f32[96,64,128]{2,1,0:T(8,128)}, s32[]{:T(128)}, s32[96]{0:T(128)}, s32[3,96]{1,0:T(4,128)S(1)}, /*index=5*/s32[]{:T(128)}, s32[]{:T...) while((s32[]{:T(128)}, f32[96,64,128]{2,1,0:T(8,128)}, ...), condition=%wide.region_8.8_spmd, body=%wide.region_6.7_spmd.sunk | while | flops 101322664 | bytes 12862631 | solution.py:47
  200.4 4.9 scatter_fusion.1
  205.3 21.8 %collective-permute-start = (bf16[192,512]{1,0:T(8,128)(2,1)S(1)}, bf16[192,512]{1,0:T(8,128)(2,1)S(1)}, u32[]{:S(2)}, u32[]{:S(2)}) collective-permute-start(bf16[192,512]{1,0:T(8,128)(2,1)S(1)} %get-tuple-element.944), channel_id=1, source_target_pairs={{448,0},{0,64},{64,128},{128,192},{192,256},{256,320},{320,384},{3... | collective-permute-start | bytes 589832 | tf_op jit(solution)/shard_map/while/body/eval_jaxpr/ppermute | solution.py:16
  230.9 11.1 %collective-permute-done = bf16[192,512]{1,0:T(8,128)(2,1)S(1)} collective-permute-done((bf16[192,512]{1,0:T(8,128)(2,1)S(1)}, bf16[192,512]{1,0:T(8,128)(2,1)S(1)}, u32[]{:S(2)}, u32[]{:S(2)}) %collective-permute-start) | collective-permute-done | bytes 196640 | tf_op jit(solution)/shard_map/while/body/eval_jaxpr/ppermute | solution.py:16
  242.2 15.7 %while.65 = (s32[]{:T(128)}, f32[96,64,128]{2,1,0:T(8,128)}, s32[]{:T(128)}, s32[96]{0:T(128)}, s32[3,96]{1,0:T(4,128)S(1)}, /*index=5*/s32[]{:T(128)}, s32[]{:T...) while((s32[]{:T(128)}, f32[96,64,128]{2,1,0:T(8,128)}, ...), condition=%wide.region_8.8_spmd, body=%wide.region_6.7_spmd.sunk | while | flops 101322664 | bytes 12862631 | solution.py:47
  253.0 4.9 scatter_fusion.1
  257.9 56.4 %collective-permute-start = (bf16[192,512]{1,0:T(8,128)(2,1)S(1)}, bf16[192,512]{1,0:T(8,128)(2,1)S(1)}, u32[]{:S(2)}, u32[]{:S(2)}) collective-permute-start(bf16[192,512]{1,0:T(8,128)(2,1)S(1)} %get-tuple-element.944), channel_id=1, source_target_pairs={{448,0},{0,64},{64,128},{128,192},{192,256},{256,320},{320,384},{3... | collective-permute-start | bytes 589832 | tf_op jit(solution)/shard_map/while/body/eval_jaxpr/ppermute | solution.py:16
  318.2 15.7 %while.65 = (s32[]{:T(128)}, f32[96,64,128]{2,1,0:T(8,128)}, s32[]{:T(128)}, s32[96]{0:T(128)}, s32[3,96]{1,0:T(4,128)S(1)}, /*index=5*/s32[]{:T(128)}, s32[]{:T...) while((s32[]{:T(128)}, f32[96,64,128]{2,1,0:T(8,128)}, ...), condition=%wide.region_8.8_spmd, body=%wide.region_6.7_spmd.sunk | while | flops 101322664 | bytes 12862631 | solution.py:47
  328.9 4.9 scatter_fusion.1
  333.9 48.8 %collective-permute-start = (bf16[192,512]{1,0:T(8,128)(2,1)S(1)}, bf16[192,512]{1,0:T(8,128)(2,1)S(1)}, u32[]{:S(2)}, u32[]{:S(2)}) collective-permute-start(bf16[192,512]{1,0:T(8,128)(2,1)S(1)} %get-tuple-element.944), channel_id=1, source_target_pairs={{448,0},{0,64},{64,128},{128,192},{192,256},{256,320},{320,384},{3... | collective-permute-start | bytes 589832 | tf_op jit(solution)/shard_map/while/body/eval_jaxpr/ppermute | solution.py:16
  386.5 15.7 %while.65 = (s32[]{:T(128)}, f32[96,64,128]{2,1,0:T(8,128)}, s32[]{:T(128)}, s32[96]{0:T(128)}, s32[3,96]{1,0:T(4,128)S(1)}, /*index=5*/s32[]{:T(128)}, s32[]{:T...) while((s32[]{:T(128)}, f32[96,64,128]{2,1,0:T(8,128)}, ...), condition=%wide.region_8.8_spmd, body=%wide.region_6.7_spmd.sunk | while | flops 101322664 | bytes 12862631 | solution.py:47
  397.3 4.9 scatter_fusion.1
  402.3 45.2 %collective-permute-start = (bf16[192,512]{1,0:T(8,128)(2,1)S(1)}, bf16[192,512]{1,0:T(8,128)(2,1)S(1)}, u32[]{:S(2)}, u32[]{:S(2)}) collective-permute-start(bf16[192,512]{1,0:T(8,128)(2,1)S(1)} %get-tuple-element.944), channel_id=1, source_target_pairs={{448,0},{0,64},{64,128},{128,192},{192,256},{256,320},{320,384},{3... | collective-permute-start | bytes 589832 | tf_op jit(solution)/shard_map/while/body/eval_jaxpr/ppermute | solution.py:16
  452.2 15.7 %while.65 = (s32[]{:T(128)}, f32[96,64,128]{2,1,0:T(8,128)}, s32[]{:T(128)}, s32[96]{0:T(128)}, s32[3,96]{1,0:T(4,128)S(1)}, /*index=5*/s32[]{:T(128)}, s32[]{:T...) while((s32[]{:T(128)}, f32[96,64,128]{2,1,0:T(8,128)}, ...), condition=%wide.region_8.8_spmd, body=%wide.region_6.7_spmd.sunk | while | flops 101322664 | bytes 12862631 | solution.py:47
  463.0 4.9 scatter_fusion.1
  468.0 43.8 %collective-permute-start = (bf16[192,512]{1,0:T(8,128)(2,1)S(1)}, bf16[192,512]{1,0:T(8,128)(2,1)S(1)}, u32[]{:S(2)}, u32[]{:S(2)}) collective-permute-start(bf16[192,512]{1,0:T(8,128)(2,1)S(1)} %get-tuple-element.944), channel_id=1, source_target_pairs={{448,0},{0,64},{64,128},{128,192},{192,256},{256,320},{320,384},{3... | collective-permute-start | bytes 589832 | tf_op jit(solution)/shard_map/while/body/eval_jaxpr/ppermute | solution.py:16
  515.7 15.7 %while.65 = (s32[]{:T(128)}, f32[96,64,128]{2,1,0:T(8,128)}, s32[]{:T(128)}, s32[96]{0:T(128)}, s32[3,96]{1,0:T(4,128)S(1)}, /*index=5*/s32[]{:T(128)}, s32[]{:T...) while((s32[]{:T(128)}, f32[96,64,128]{2,1,0:T(8,128)}, ...), condition=%wide.region_8.8_spmd, body=%wide.region_6.7_spmd.sunk | while | flops 101322664 | bytes 12862631 | solution.py:47
  526.5 4.9 scatter_fusion.1
  533.9 14.7 %scatter_fusion.2 = f32[128,64,128]{2,1,0:T(8,128)} fusion(f32[128,64,128]{2,1,0:T(8,128)} %broadcast_in_dim.73, s32[96]{0:T(128)S(1)} %copy-done.11, f32[96,64,128]{2,1,0:T(8,128)} %get-tuple-element.516), kind=kCustom, calls=%fused_computation.10 | custom fusion | bytes 9437568 | tf_op jit(solution)/shard_map/scatter | solution.py:63
  548.6 65.7 %all-to-all-start = ((f32[64,2,64,128]{3,2,1,0:T(8,128)}), f32[64,2,64,128]{3,2,1,0:T(8,128)}, u32[]{:S(2)}, u32[]{:S(2)}) async-start(f32[64,2,64,128]{3,2,1,0:T(8,128)} %bitcast.79), calls=%async_computation | async-start | bytes 8388608 | tf_op jit(solution)/shard_map/all_to_all | solution.py:111
  614.8 23.0 %scatter_custom_fusion.2 = s32[128]{0:T(128)S(1)} fusion(s32[6144]{0:T(1024)S(1)} %bitcast.82, s32[6144]{0:T(1024)S(1)} %reshape.362, s32[]{:T(128)} %constant.281.clone.1), kind=kCustom, calls=%fused_computation.94 | custom fusion | bytes 516 | tf_op jit(solution)/shard_map/scatter | solution.py:73
  637.8 162.3 %all-to-all-done = f32[64,2,64,128]{3,2,1,0:T(8,128)} async-done(((f32[64,2,64,128]{3,2,1,0:T(8,128)}), f32[64,2,64,128]{3,2,1,0:T(8,128)}, u32[]{:S(2)}, u32[]{:S(2)}) %all-to-all-start) | async-done | bytes 4194336 | tf_op jit(solution)/shard_map/all_to_all | solution.py:111
  800.2 13.5 %scatter_fusion.3 = f32[32,64,128]{2,1,0:T(8,128)S(1)} fusion(f32[32,64,128]{2,1,0:T(8,128)S(1)} %broadcast_in_dim.69, s32[128]{0:T(128)S(1)} %compare_select_fusion.12, f32[128,64,128]{2,1,0:T(8,128)} %bitcast.22), kind=kCustom, calls=%fused_computation.11 | custom fusion | flops 1048576 | bytes 12583424 | tf_op jit(solution)/shard_map/scatter-add | solution.py:75
  814.9 108.6 %reduce-scatter.2.cloned.1.call-done = f32[8,8,512]{2,1,0:T(8,128)} async-done(((f32[8,64,512]{2,1,0:T(8,128)}), f32[8,8,512]{2,1,0:T(8,128)}) %reduce-scatter.2.cloned.1.call-update) | async-done | bytes 131088 | tf_op jit(solution)/shard_map/reduce_scatter | solution.py:113
  (232 shorter events, 135.4 us)
Async XLA Ops:
  6.5 23.2 %copy-start = (s32[256]{0:T(256)S(1)}, s32[256]{0:T(256)}, u32[]{:S(2)}) copy-start(s32[256]{0:T(256)} %param.19) | copy-start | bytes 3076
  7.5 2.4 copy-start.3
  7.5 7.2 copy-start.1
  29.7 38.6 %copy-start.10 = (s32[64,96]{1,0:T(8,128)S(1)}, s32[64,96]{1,0:T(8,128)}, u32[]{:S(2)}) copy-start(s32[64,96]{1,0:T(8,128)} %param.18) | copy-start | bytes 73732
  29.7 42.2 %copy-start.4 = (bf16[192,512]{1,0:T(8,128)(2,1)S(1)}, bf16[192,512]{1,0:T(8,128)(2,1)}, u32[]{:S(2)}) copy-start(bf16[192,512]{1,0:T(8,128)(2,1)} %copy-done.3) | copy-start | bytes 589828
  68.3 3.7 copy-start.5
  71.4 0.6 copy-start.7
  72.0 55.9 %collective-permute-start = (bf16[192,512]{1,0:T(8,128)(2,1)S(1)}, bf16[192,512]{1,0:T(8,128)(2,1)S(1)}, u32[]{:S(2)}, u32[]{:S(2)}) collective-permute-start(bf16[192,512]{1,0:T(8,128)(2,1)S(1)} %get-tuple-element.944), channel_id=1, source_target_pairs={{448,0},{0,64},{64,128},{128,192},{192,256},{256,320},{320,384},{3... | collective-permute-start | bytes 589832 | tf_op jit(solution)/shard_map/while/body/eval_jaxpr/ppermute | solution.py:16
  133.3 0.7 copy-start.2
  143.7 45.9 %collective-permute-start = (bf16[192,512]{1,0:T(8,128)(2,1)S(1)}, bf16[192,512]{1,0:T(8,128)(2,1)S(1)}, u32[]{:S(2)}, u32[]{:S(2)}) collective-permute-start(bf16[192,512]{1,0:T(8,128)(2,1)S(1)} %get-tuple-element.944), channel_id=1, source_target_pairs={{448,0},{0,64},{64,128},{128,192},{192,256},{256,320},{320,384},{3... | collective-permute-start | bytes 589832 | tf_op jit(solution)/shard_map/while/body/eval_jaxpr/ppermute | solution.py:16
  195.0 0.7 copy-start.2
  205.3 36.7 %collective-permute-start = (bf16[192,512]{1,0:T(8,128)(2,1)S(1)}, bf16[192,512]{1,0:T(8,128)(2,1)S(1)}, u32[]{:S(2)}, u32[]{:S(2)}) collective-permute-start(bf16[192,512]{1,0:T(8,128)(2,1)S(1)} %get-tuple-element.944), channel_id=1, source_target_pairs={{448,0},{0,64},{64,128},{128,192},{192,256},{256,320},{320,384},{3... | collective-permute-start | bytes 589832 | tf_op jit(solution)/shard_map/while/body/eval_jaxpr/ppermute | solution.py:16
  247.5 0.7 copy-start.2
  257.9 60.2 %collective-permute-start = (bf16[192,512]{1,0:T(8,128)(2,1)S(1)}, bf16[192,512]{1,0:T(8,128)(2,1)S(1)}, u32[]{:S(2)}, u32[]{:S(2)}) collective-permute-start(bf16[192,512]{1,0:T(8,128)(2,1)S(1)} %get-tuple-element.944), channel_id=1, source_target_pairs={{448,0},{0,64},{64,128},{128,192},{192,256},{256,320},{320,384},{3... | collective-permute-start | bytes 589832 | tf_op jit(solution)/shard_map/while/body/eval_jaxpr/ppermute | solution.py:16
  323.5 0.7 copy-start.2
  333.9 52.5 %collective-permute-start = (bf16[192,512]{1,0:T(8,128)(2,1)S(1)}, bf16[192,512]{1,0:T(8,128)(2,1)S(1)}, u32[]{:S(2)}, u32[]{:S(2)}) collective-permute-start(bf16[192,512]{1,0:T(8,128)(2,1)S(1)} %get-tuple-element.944), channel_id=1, source_target_pairs={{448,0},{0,64},{64,128},{128,192},{192,256},{256,320},{320,384},{3... | collective-permute-start | bytes 589832 | tf_op jit(solution)/shard_map/while/body/eval_jaxpr/ppermute | solution.py:16
  391.9 0.7 copy-start.2
  402.3 49.9 %collective-permute-start = (bf16[192,512]{1,0:T(8,128)(2,1)S(1)}, bf16[192,512]{1,0:T(8,128)(2,1)S(1)}, u32[]{:S(2)}, u32[]{:S(2)}) collective-permute-start(bf16[192,512]{1,0:T(8,128)(2,1)S(1)} %get-tuple-element.944), channel_id=1, source_target_pairs={{448,0},{0,64},{64,128},{128,192},{192,256},{256,320},{320,384},{3... | collective-permute-start | bytes 589832 | tf_op jit(solution)/shard_map/while/body/eval_jaxpr/ppermute | solution.py:16
  457.6 0.7 copy-start.2
  468.0 47.6 %collective-permute-start = (bf16[192,512]{1,0:T(8,128)(2,1)S(1)}, bf16[192,512]{1,0:T(8,128)(2,1)S(1)}, u32[]{:S(2)}, u32[]{:S(2)}) collective-permute-start(bf16[192,512]{1,0:T(8,128)(2,1)S(1)} %get-tuple-element.944), channel_id=1, source_target_pairs={{448,0},{0,64},{64,128},{128,192},{192,256},{256,320},{320,384},{3... | collective-permute-start | bytes 589832 | tf_op jit(solution)/shard_map/while/body/eval_jaxpr/ppermute | solution.py:16
  521.0 0.7 copy-start.2
  531.4 2.5 copy-start.11
  548.6 65.8 %copy-start.8 = (s32[64,96]{1,0:T(8,128)S(1)}, s32[64,96]{1,0:T(8,128)}, u32[]{:S(2)}) copy-start(s32[64,96]{1,0:T(8,128)} %copy-done.7) | copy-start | bytes 73732
  548.6 66.0 %copy-start.9 = (s32[64,96]{1,0:T(8,128)S(1)}, s32[64,96]{1,0:T(8,128)}, u32[]{:S(2)}) copy-start(s32[64,96]{1,0:T(8,128)} %get-tuple-element.651) | copy-start | bytes 73732
  548.6 66.1 %copy-start.6 = (s32[6144]{0:T(1024)S(1)}, s32[6144]{0:T(1024)}, u32[]{:S(2)}) copy-start(s32[6144]{0:T(1024)} %copy-done.5) | copy-start | bytes 73732
  548.6 251.5 %all-to-all-start = ((f32[64,2,64,128]{3,2,1,0:T(8,128)}), f32[64,2,64,128]{3,2,1,0:T(8,128)}, u32[]{:S(2)}, u32[]{:S(2)}) async-start(f32[64,2,64,128]{3,2,1,0:T(8,128)} %bitcast.79), calls=%async_computation | async-start | bytes 8388608 | tf_op jit(solution)/shard_map/all_to_all | solution.py:111
  614.3 309.2 %reduce-scatter.2.cloned.1.call-start = ((), (), s32[]{:S(2)}) async-start(), calls=%async_computation.2 | async-start | bytes 1179648 | tf_op jit(solution)/shard_map/reduce_scatter | solution.py:113
Sparse Core Ops, SparseCore 0:
  815.0 108.4 reduce-scatter.1
where the time goes:
time: 939 us; the launch traced here: 932 us
  starting transfers between devices  350 us (37%)
  waiting for transfers between devices  308 us (33%)
  local copies, waits for them, and re-layouts  160 us (17%)
  other arithmetic  70.9 us (8%)
  matrix products  22.4 us (2%)
  between operations  14.4 us (2%)
    ppermute x7, starting transfers between devices, from_behind(): return lax.ppermute(block, axis, route)  285 us
    all_to_all x1, waiting for transfers between devices, shards(): lax.all_to_all(outgoing, 'ao', split_axis=0, concat_axis=0, tiled=True)  162 us
    reduce_scatter x1, waiting for transfers between devices, shards(): result = lax.psum_scatter(summed, 'fit', scatter_dimension=1, tiled=True)  109 us
    all_to_all x1, starting transfers between devices, shards(): lax.all_to_all(outgoing, 'ao', split_axis=0, concat_axis=0, tiled=True)  65.7 us
    scatter-add x8, other arithmetic, one_block(): return running.at[tile_ids].add(product)  39.2 us
    gather x2, local copies, waits for them, and re-layouts, routing(): slot_ids = owner_slot[tile_list // occ_count]  38.6 us
    ppermute x7, waiting for transfers between devices, from_behind(): return lax.ppermute(block, axis, route)  37.5 us
    gather x16, local copies, waits for them, and re-layouts, one_block(): picked = resident[cycle_step * pair_step + jnp.maximum(pair_ids, 0)]  29.1 us
  transfers between devices with their start and end apart: 9, of which 6 were waited for; matrix products, arithmetic and copies ran while one was open for 5% of the time, Pallas kernels for 0%

commit v1 on v0

v1 whole, which is shorter than its diff:
```python
import functools

import jax
import jax.numpy as jnp
from jax import lax
from jax.experimental import pallas as pl
from jax.experimental.pallas import tpu as pltpu
from jax.sharding import PartitionSpec as P

AB = 64
FB = 64
OB = 128
OWN_CAP = 8
CAP = 2
NY = 4
NZH = 2
NZL = 8
NXC = 8
UNROLL = 8
MESH = pl.DeviceIdType.MESH
TOP = 32767.0
TINY = 1e-30


def gather_kernel(x_ref, out_ref, send_own, recv_own, send_z, recv_z, send_fw, recv_fw, local_sem):
    fit = lax.axis_index("fit")
    ao = lax.axis_index("ao")
    y, zh = fit // NZH, fit % NZH
    partner = y * NZH + (1 - zh)
    barrier = pltpu.get_barrier_semaphore()
    for d in range(1, NY):
        pl.semaphore_signal(barrier, inc=1, device_id=(((y + d) % NY) * NZH + zh, ao), device_id_type=MESH)
    pl.semaphore_signal(barrier, inc=1, device_id=(partner, ao), device_id_type=MESH)
    pl.semaphore_wait(barrier, NY)

    blocks = x_ref.shape[0] // FB
    across = []
    for j in range(blocks):
        copy = pltpu.make_async_remote_copy(
            src_ref=x_ref.at[pl.ds(j * FB, FB)],
            dst_ref=out_ref.at[fit, pl.ds(j * FB, FB)],
            send_sem=send_z.at[j],
            recv_sem=recv_z.at[j],
            device_id=(partner, ao),
            device_id_type=MESH,
        )
        copy.start()
        across.append(copy)
    own = []
    for d in range(1, NY):
        copy = pltpu.make_async_remote_copy(
            src_ref=x_ref,
            dst_ref=out_ref.at[fit],
            send_sem=send_own.at[d - 1],
            recv_sem=recv_own.at[d - 1],
            device_id=(((y + d) % NY) * NZH + zh, ao),
            device_id_type=MESH,
        )
        copy.start()
        own.append(copy)
    local = pltpu.make_async_copy(x_ref, out_ref.at[fit], local_sem)
    local.start()
    forward = []
    for j in range(blocks):
        across[j].wait_recv()
        for d in range(1, NY):
            copy = pltpu.make_async_remote_copy(
                src_ref=out_ref.at[partner, pl.ds(j * FB, FB)],
                dst_ref=out_ref.at[partner, pl.ds(j * FB, FB)],
                send_sem=send_fw.at[j, d - 1],
                recv_sem=recv_fw.at[j, d - 1],
                device_id=(((y + d) % NY) * NZH + zh, ao),
                device_id_type=MESH,
            )
            copy.start()
            forward.append(copy)
    local.wait()
    for copy in own:
        copy.wait()
    for copy in forward:
        copy.wait()
    for copy in across:
        copy.wait_send()


def gather_occ(occ):
    blocks = occ.shape[0] // FB
    return pl.pallas_call(
        gather_kernel,
        out_shape=jax.ShapeDtypeStruct((NY * NZH,) + occ.shape, occ.dtype),
        in_specs=[pl.BlockSpec(memory_space=pltpu.VMEM)],
        out_specs=pl.BlockSpec(memory_space=pltpu.VMEM),
        scratch_shapes=[
            pltpu.SemaphoreType.DMA((NY - 1,)),
            pltpu.SemaphoreType.DMA((NY - 1,)),
            pltpu.SemaphoreType.DMA((blocks,)),
            pltpu.SemaphoreType.DMA((blocks,)),
            pltpu.SemaphoreType.DMA((blocks, NY - 1)),
            pltpu.SemaphoreType.DMA((blocks, NY - 1)),
            pltpu.SemaphoreType.DMA,
        ],
        compiler_params=pltpu.CompilerParams(collective_id=0, has_side_effects=True, vmem_limit_bytes=16 << 20),
        name="gather_occ",
    )(occ)


def product_kernel(fit_ref, count_ref, list_ref, occ_ref, res_ref, acc_ref, wide):
    fits, rows, occ_width = occ_ref.shape
    blocks, occs = rows // FB, occ_width // OB
    pairs = list_ref.shape[1]
    per_step = res_ref.shape[0] // fits
    wide[...] = jnp.zeros_like(wide)
    acc_ref[...] = jnp.zeros_like(acc_ref)

    def spread(h, _):
        for j in range(blocks):
            for o in range(occs):
                piece = occ_ref[h, j * FB : (j + 1) * FB, o * OB : (o + 1) * OB]
                at = h * (blocks * occs) + j * occs + o
                wide[at, :FB, :OB] = piece
                wide[at, FB:, OB:] = piece
        return 0

    lax.fori_loop(0, fits, spread, 0)
    fit = fit_ref[0]

    def step(s, _):
        base = ((fit - s + fits) % fits) * (blocks * occs)

        def some(i, _):
            done = []
            for u in range(UNROLL):
                code = list_ref[s, i * UNROLL + u]
                a = res_ref[s * per_step + (code & 31)]
                b = wide[base + ((code >> 5) & 15)]
                done.append((code >> 9, jnp.dot(a, b, preferred_element_type=jnp.float32)))
            for t, value in done:
                parts = []
                for y in range(NY):
                    parts.append(value[y * 8 : y * 8 + 8, :OB])
                    parts.append(value[y * 8 : y * 8 + 8, OB:])
                acc_ref[t] += jnp.concatenate(parts, axis=0)
            return 0

        lax.fori_loop(0, (count_ref[s] + UNROLL - 1) // UNROLL, some, 0)
        return 0

    lax.fori_loop(0, fits, step, 0)


def products(fit, counts, codes, occ_all, resident, tiles):
    fits, rows, occ_width = occ_all.shape
    weights = fits * (rows // FB) * (occ_width // OB)
    return pl.pallas_call(
        product_kernel,
        out_shape=jax.ShapeDtypeStruct((tiles + 1, AB, OB), jnp.float32),
        in_specs=[
            pl.BlockSpec(memory_space=pltpu.SMEM),
            pl.BlockSpec(memory_space=pltpu.SMEM),
            pl.BlockSpec(memory_space=pltpu.SMEM),
            pl.BlockSpec(memory_space=pltpu.VMEM),
            pl.BlockSpec(memory_space=pltpu.VMEM),
        ],
        out_specs=pl.BlockSpec(memory_space=pltpu.VMEM),
        scratch_shapes=[pltpu.VMEM((weights, 2 * FB, 2 * OB), jnp.bfloat16)],
        compiler_params=pltpu.CompilerParams(vmem_limit_bytes=32 << 20),
        name="products",
    )(fit, counts, codes, occ_all, resident)


def coded(values):
    top = jnp.maximum(jnp.max(jnp.max(jnp.abs(values), axis=0), axis=0, keepdims=True), TINY)
    whole = jnp.round(values * (TOP / top)[None])
    return whole.astype(jnp.int32).astype(jnp.int16), top * (1.0 / TOP)


def decoded(whole):
    return whole.astype(jnp.int32).astype(jnp.float32)


def reduce_kernel(
    index_ref, acc_ref, target_ref, out_ref,
    qy, sy, ry, rsy, summed, qa, sa, ra, rsa, rb, rsb, flat, final,
    send_y, recv_y, send_a, recv_a, send_b, recv_b,
):
    fit = lax.axis_index("fit")
    ao = lax.axis_index("ao")
    y, zh = fit // NZH, fit % NZH
    zl, xc = ao // NXC, ao % NXC
    z = zh * NZL + zl
    nz = NZH * NZL
    groups = summed.shape[0] // 8

    def at_y(d):
        return (((y + d) % NY) * NZH + zh, ao)

    def at_z(d):
        other = (z + d) % nz
        return other, (y * NZH + other // NZL, (other % NZL) * NXC + xc)

    def at_x(d):
        other = (xc + d) % NXC
        return other, (fit, zl * NXC + other)

    barrier = pltpu.get_barrier_semaphore()
    for d in range(1, NY):
        pl.semaphore_signal(barrier, inc=1, device_id=at_y(d), device_id_type=MESH)
    for d in range(1, nz):
        pl.semaphore_signal(barrier, inc=1, device_id=at_z(d)[1], device_id_type=MESH)
    for d in range(1, NXC):
        pl.semaphore_signal(barrier, inc=1, device_id=at_x(d)[1], device_id_type=MESH)

    copies_y = []
    for d in range(1, NY):
        at = pl.multiple_of(((y + d) % NY) * 16, 16)

        def code_group(g, _, at=at, d=d):
            whole, scale = coded(acc_ref[pl.ds(g * 8, 8), pl.ds(at, 16), :])
            qy[d - 1, pl.ds(g * 8, 8)] = whole
            sy[d - 1, g] = scale
            return 0

        lax.fori_loop(0, groups, code_group, 0)
        if d == 1:
            pl.semaphore_wait(barrier, NY - 1 + nz - 1 + NXC - 1)
        for n, (src, dst) in enumerate(((qy, ry), (sy, rsy))):
            copy = pltpu.make_async_remote_copy(
                src_ref=src.at[d - 1],
                dst_ref=dst.at[d - 1],
                send_sem=send_y.at[n, d - 1],
                recv_sem=recv_y.at[n, d - 1],
                device_id=at_y(d),
                device_id_type=MESH,
            )
            copy.start()
            copies_y.append(copy)
    for copy in copies_y:
        copy.wait_recv()

    mine = pl.multiple_of(y * 16, 16)

    def add_group(g, _):
        total = acc_ref[pl.ds(g * 8, 8), pl.ds(mine, 16), :]
        for d in range(NY - 1):
            total = total + decoded(ry[d, pl.ds(g * 8, 8)]) * rsy[d, g][None]
        summed[pl.ds(g * 8, 8)] = total
        return 0

    lax.fori_loop(0, groups, add_group, 0)

    lower = lax.broadcasted_iota(jnp.int32, (8, OB), 0) < 4

    def pack(block, _):
        firsts, seconds = [], []
        for other in range(NXC):
            halves = ([], [])
            for rank in range(CAP):
                tile = summed[index_ref[(block * NXC + other) * CAP + rank]]
                a, b = tile[:8], tile[8:]
                halves[0].append(jnp.where(lower, a, pltpu.roll(b, 4, 0)))
                halves[1].append(jnp.where(lower, pltpu.roll(a, 4, 0), b))
            firsts.append(jnp.concatenate(halves[0], axis=0)[None])
            seconds.append(jnp.concatenate(halves[1], axis=0)[None])
        for half, values in enumerate((firsts, seconds)):
            whole, scale = coded(jnp.concatenate(values, axis=0))
            qa[half * NZL + block] = whole
            sa[half * NZL + block] = scale
        return 0

    lax.fori_loop(0, NZL, pack, 0)

    copies_a = []
    for d in range(1, nz):
        other, device = at_z(d)
        for n, (src, dst) in enumerate(((qa, ra), (sa, rsa))):
            copy = pltpu.make_async_remote_copy(
                src_ref=src.at[other],
                dst_ref=dst.at[z],
                send_sem=send_a.at[n, d - 1],
                recv_sem=recv_a.at[n, d - 1],
                device_id=device,
                device_id_type=MESH,
            )
            copy.start()
            copies_a.append(copy)
    ra[z] = qa[z]
    rsa[z] = sa[z]
    for copy in copies_a:
        copy.wait_recv()

    copies_b = []
    for d in range(1, NXC):
        other, device = at_x(d)
        for n, (src, dst) in enumerate(((ra.at[:, other], rb.at[xc]), (rsa, rsb.at[xc]))):
            copy = pltpu.make_async_remote_copy(
                src_ref=src,
                dst_ref=dst,
                send_sem=send_b.at[n, d - 1],
                recv_sem=recv_b.at[n, d - 1],
                device_id=device,
                device_id_type=MESH,
            )
            copy.start()
            copies_b.append(copy)
    rb[xc] = ra[:, xc]
    rsb[xc] = rsa[...]
    for copy in copies_b:
        copy.wait_recv()

    def spread(source, _):
        for k in range(nz):
            value = decoded(rb[source, k]) * rsb[source, k]
            flat[pl.ds(pl.multiple_of((source * nz + k) * 16, 16), 16), :] = value
        return 0

    lax.fori_loop(0, NXC, spread, 0)
    entries = NXC * nz * CAP
    occs = out_ref.shape[2] // OB
    names = lax.broadcasted_iota(jnp.int32, (occs * OWN_CAP, entries), 0)
    select = (names == target_ref[...]).astype(jnp.float32)
    for m in range(8):
        part = jnp.dot(
            select, flat[pl.ds(m, entries, stride=8), :],
            precision=lax.Precision.HIGHEST, preferred_element_type=jnp.float32,
        )
        row = 2 * (m % 4) + m // 4
        for o in range(occs):
            final[o, pl.ds(row, OWN_CAP, stride=8), :] = part[o * OWN_CAP : (o + 1) * OWN_CAP]
    for o in range(occs):
        out_ref[:, :, o * OB : (o + 1) * OB] = final[o].reshape(OWN_CAP, 8, OB).astype(out_ref.dtype)
    for copy in copies_y + copies_a + copies_b:
        copy.wait_send()


def reduce_tiles(index, acc, target, occ_width, tiles):
    nz = NZH * NZL
    i16, f32 = jnp.int16, jnp.float32
    return pl.pallas_call(
        reduce_kernel,
        out_shape=jax.ShapeDtypeStruct((OWN_CAP, AB // (NY * NZH), occ_width), jnp.bfloat16),
        in_specs=[
            pl.BlockSpec(memory_space=pltpu.SMEM),
            pl.BlockSpec(memory_space=pltpu.VMEM),
            pl.BlockSpec(memory_space=pltpu.VMEM),
        ],
        out_specs=pl.BlockSpec(memory_space=pltpu.VMEM),
        scratch_shapes=[
            pltpu.VMEM((NY - 1, tiles, 16, OB), i16),
            pltpu.VMEM((NY - 1, tiles // 8, 1, OB), f32),
            pltpu.VMEM((NY - 1, tiles, 16, OB), i16),
            pltpu.VMEM((NY - 1, tiles // 8, 1, OB), f32),
            pltpu.VMEM((tiles, 16, OB), f32),
            pltpu.VMEM((nz, NXC, 16, OB), i16),
            pltpu.VMEM((nz, 1, OB), f32),
            pltpu.VMEM((nz, NXC, 16, OB), i16),
            pltpu.VMEM((nz, 1, OB), f32),
            pltpu.VMEM((NXC, nz, 16, OB), i16),
            pltpu.VMEM((NXC, nz, 1, OB), f32),
            pltpu.VMEM((NXC * nz * 16, OB), f32),
            pltpu.VMEM((occ_width // OB, OWN_CAP * 8, OB), f32),
            pltpu.SemaphoreType.DMA((2, NY - 1)),
            pltpu.SemaphoreType.DMA((2, NY - 1)),
            pltpu.SemaphoreType.DMA((2, nz - 1)),
            pltpu.SemaphoreType.DMA((2, nz - 1)),
            pltpu.SemaphoreType.DMA((2, NXC - 1)),
            pltpu.SemaphoreType.DMA((2, NXC - 1)),
        ],
        compiler_params=pltpu.CompilerParams(collective_id=1, has_side_effects=True, vmem_limit_bytes=32 << 20),
        name="reduce_tiles",
    )(index, acc, target)


def before(n):
    at = jnp.arange(n)
    return (at[:, None] < at[None, :]).astype(jnp.float32)


def pair_list(row_tiles, row_pairs, live_rows, tile_occ):
    blocks, steps, width = row_pairs.shape
    tiles = tile_occ.shape[0]
    usable = (row_pairs >= 0) & (jnp.arange(width) < live_rows[:, None])[None]
    occ_of = jnp.sum(jnp.where(row_tiles[:, :, None] == jnp.arange(tiles), tile_occ, 0), axis=2)
    kinds = jnp.arange(blocks)[:, None, None] * 4 + occ_of[None]
    codes = row_pairs + 32 * kinds + 512 * row_tiles[None]
    usable = usable.transpose(1, 0, 2).reshape(steps, blocks * width)
    codes = codes.transpose(1, 0, 2).reshape(steps, blocks * width)
    place = jnp.dot(usable.astype(jnp.float32), before(blocks * width)).astype(jnp.int32)
    place = jnp.where(usable, place, -1)
    slots = jnp.arange(blocks * width)
    listed = jnp.sum(jnp.where(place[:, None, :] == slots[None, :, None], codes[:, None, :], 0), axis=2)
    counts = jnp.sum(usable.astype(jnp.int32), axis=1)
    return counts, jnp.where(slots[None] < counts[:, None], listed, 512 * tiles)


def routing(tile_list, codes, owner_slot, column, occs):
    blocks = owner_slot.shape[0]
    tiles = codes.shape[0]
    ao_count = tile_list.shape[0]
    numbers = jnp.arange(blocks)
    slots = jnp.sum(jnp.where((codes // occs)[:, None] == numbers, owner_slot, 0), axis=1)
    owners = slots // OWN_CAP
    at = jnp.arange(tiles)
    ranks = jnp.sum(((owners[:, None] == owners[None, :]) & (at[None, :] < at[:, None])).astype(jnp.int32), axis=1)
    places = owners * CAP + ranks
    index = jnp.sum(jnp.where(places[None, :] == jnp.arange(ao_count * CAP)[:, None], at[None, :], 0), axis=1)

    mine = column * OWN_CAP + jnp.arange(OWN_CAP)
    held = jnp.sum(jnp.where(owner_slot[None, :] == mine[:, None], numbers[None, :] + 1, 0), axis=1) - 1
    names = tile_list // occs
    slot = jnp.sum(
        jnp.where(names[:, :, None] == held[None, None, :], jnp.arange(OWN_CAP) + 1, 0), axis=2
    ) - 1
    owned = slot >= 0
    goal = (tile_list % occs) * OWN_CAP + slot
    rank = jnp.dot(owned.astype(jnp.float32), before(tiles)).astype(jnp.int32)
    target = jnp.stack(
        [jnp.sum(jnp.where(owned & (rank == r), goal + 1, 0), axis=1) - 1 for r in range(CAP)], axis=1
    )
    target = target.reshape(NZL, NXC, CAP).transpose(1, 0, 2)
    target = jnp.broadcast_to(target[:, None], (NXC, NZH, NZL, CAP))
    return index, target.reshape(1, -1)


def shards(occ_blocks, resident, row_tiles, row_pairs, live_rows, tile_list, owner_slot):
    column = lax.axis_index("ao")
    fit = lax.axis_index("fit")
    occs = occ_blocks.shape[1] // OB
    codes = lax.dynamic_index_in_dim(tile_list, column, 0, keepdims=False)
    tiles = codes.shape[0]
    counts, listed = pair_list(row_tiles[0], row_pairs[:, 0], live_rows[0], codes % occs)
    index, target = routing(tile_list, codes, owner_slot, column, occs)
    occ_all = gather_occ(occ_blocks)
    rows = resident.reshape(resident.shape[0], AB // 2, 2 * FB)
    acc = products(fit.reshape(1), counts, listed, occ_all, rows, tiles)
    return reduce_tiles(index, acc, target, occ_blocks.shape[1], tiles)


def solution(mesh):
    return jax.shard_map(
        shards,
        mesh=mesh,
        in_specs=(
            P(("fit", "ao"), None),
            P(("fit", "ao"), None),
            P(("fit", "ao"), None, None),
            P(None, ("fit", "ao"), None, None),
            P(("fit", "ao"), None),
            P(),
            P(),
        ),
        out_specs=P("ao", "fit", None),
        check_vma=False,
    )
```

time: 939 us -> 131 us (0.14)
  starting transfers between devices: 350 us -> 0 us
  waiting for transfers between devices: 308 us -> 0 us
  local copies, waits for them, and re-layouts: 160 us -> 4.27 us
  Pallas kernels: 0 us -> 118 us
  other arithmetic: 70.9 us -> 7.6 us
  matrix products: 22.4 us -> 0.38 us
  between operations: 14.4 us -> 0.18 us
    ppermute x7 -> x0, starting transfers between devices: 285 us -> none  [from_behind(): return lax.ppermute(block, axis, route)]
    all_to_all x1 -> x0, waiting for transfers between devices: 162 us -> none  [shards(): lax.all_to_all(outgoing, 'ao', split_axis=0, concat_axis=0, tiled=True)]
    pallas_call x0 -> x3, Pallas kernels: none -> 118 us  [the longest x1 72.4 us: reduce_tiles(): pl.pallas_call(reduce_kernel, out_shape=jax.ShapeDtypeStruct((OWN_CAP, AB...]
    reduce_scatter x1 -> x0, waiting for transfers between devices: 109 us -> none  [shards(): result = lax.psum_scatter(summed, 'fit', scatter_dimension=1, tiled=True)]
    gather x34 -> x0, local copies, waits for them, and re-layouts: 88.5 us -> none  [the longest x2 38.6 us: routing(): slot_ids = owner_slot[tile_list // occ_count]]
    all_to_all x1 -> x0, starting transfers between devices: 65.7 us -> none  [shards(): lax.all_to_all(outgoing, 'ao', split_axis=0, concat_axis=0, tiled=True)]
    scatter-add x9 -> x0, other arithmetic: 52.7 us -> none  [the longest x8 39.2 us: one_block(): return running.at[tile_ids].add(product)]
    scatter x2 -> x0, local copies, waits for them, and re-layouts: 37.6 us -> none  [the longest x1 23 us: unpack(): target_at.at[position.reshape(-1)].set(targets.reshape(-1), mode='drop')]
  transfers between devices with their start and end apart: 9 -> 0, of which waited for: 6 -> 0; matrix products, arithmetic and copies ran while one was open for 5% -> 0% of each run, Pallas kernels for 0% -> 0%
where the time goes in v1:
time: 131 us; the launch traced here: 130 us
  Pallas kernels  118 us (90%)
  other arithmetic  7.6 us (6%)
  local copies, waits for them, and re-layouts  4.27 us (3%)
    pallas_call x1, Pallas kernels, reduce_tiles(): pl.pallas_call(reduce_kernel, out_shape=jax.ShapeDtypeStruct((OWN_CAP, AB...  72.4 us
    pallas_call x1, Pallas kernels, gather_occ(): pl.pallas_call(gather_kernel, out_shape=jax.ShapeDtypeStruct((NY * NZH,)...  35 us
    pallas_call x1, Pallas kernels, products(): pl.pallas_call(product_kernel, out_shape=jax.ShapeDtypeStruct((tiles + 1,...  10.4 us
    unnamed x8, local copies, waits for them, and re-layouts  3.64 us

profile of v1, /device:TPU:1, one launch (start us, length us, event | category | flops | bytes accessed | tf_op | source)
XLA Modules:
  0.0 130.2 jit_solution(17863188002336516609)
XLA Ops:
  0.0 0.7 and_select_fusion
  0.7 0.7 and_select_fusion.2
  1.4 0.9 select_reduce_fusion.3
  2.3 0.2 convert_reduce_fusion
  2.5 0.1 select_reduce_fusion.4.index_ref
  2.6 0.7 iota_compare_fusion.10
  3.3 0.8 convert_reduce_fusion.1
  4.1 0.7 multiply_bitcast_fusion
  4.8 1.0 select_reduce_fusion.1
  5.9 0.8 fusion.8
  6.7 0.1 broadcast_in_dim.112
  6.8 0.1 reshape.155
  6.9 0.1 fusion
  7.0 0.5 select_reduce_fusion
  7.5 0.1 fusion.9.list_ref
  7.6 0.9 copy-done
  8.5 35.0 %gather_occ.1.occ_ref = bf16[8,192,512]{2,1,0:T(8,128)(2,1)S(1)} custom-call(bf16[192,512]{1,0:T(8,128)(2,1)S(1)} %copy-done), custom_call_target="tpu_custom_call" | custom-call | tf_op jit(solution)/shard_map/gather_occ/pallas_call | solution.py:88
  43.5 2.1 %copy.16 = bf16[32,8,32,128]{3,2,1,0:T(8,128)(2,1)S(1)} copy(bf16[32,8,32,128]{3,1,2,0:T(8,128)(2,1)} %bitcast.42) | data formatting | bytes 4194304
  45.6 0.0 copy-start.2
  45.6 0.0 copy-start.1
  45.6 10.4 %products.1.acc_ref = f32[97,64,128]{2,1,0:T(8,128)S(1)} custom-call(s32[1]{0:T(128)} %bitcast.1.fit_ref, s32[8]{0:T(128)S(1)} %get-tuple-element.9.count_ref, s32[8,288]{1,0:T(8,128)S(1)} %fusion.9.list_ref, bf16[8,192,512]{2,1,0:T(8,128)(2,1)S(1)} %gather_occ.1.occ_ref, bf16[256,32,128]{2,1,0:T(8,128)(2,1)S(1)} %bitcast.41), custom_call_target="tpu_custom_call" | custom-call | tf_op jit(solution)/shard_map/products/pallas_call | solution.py:154
  56.1 0.0 copy-done.2
  56.1 0.2 select_reduce_fusion.7
  56.3 0.0 copy-done.1
  56.3 0.2 select_reduce_fusion.2
  56.5 0.2 select_reduce_fusion.6
  56.7 0.1 sub.40
  56.8 0.1 sub.38
  56.9 0.1 copy.15
  57.0 0.1 reshape.157.target_ref
  57.2 72.4 %reduce_tiles.1 = bf16[8,8,512]{2,1,0:T(8,128)(2,1)S(1)} custom-call(s32[128]{0:T(128)S(1)} %select_reduce_fusion.4.index_ref, f32[97,64,128]{2,1,0:T(8,128)S(1)} %products.1.acc_ref, s32[1,256]{1,0:T(1,128)S(1)} %reshape.157.target_ref), custom_call_target="tpu_custom_call" | custom-call | tf_op jit(solution)/shard_map/reduce_tiles/pallas_call | solution.py:338
  129.6 0.6 copy.18
  (14 shorter events, 0.1 us)
Async XLA Ops:
  7.6 0.9 copy-start
  45.6 10.4 %copy-start.2 = (s32[256]{0:T(256)S(1)}, s32[256]{0:T(256)}, u32[]{:S(2)}) copy-start(s32[256]{0:T(256)} %param.13) | copy-start | bytes 3076
  45.6 10.6 %copy-start.1 = (s32[64,96]{1,0:T(8,128)S(1)}, s32[64,96]{1,0:T(8,128)}, u32[]{:S(2)}) copy-start(s32[64,96]{1,0:T(8,128)} %param.12) | copy-start | bytes 73732

commit v2 on v0

v2 whole, which is shorter than its diff:
```python
import functools

import jax
import jax.numpy as jnp
from jax import lax
from jax.experimental import pallas as pl
from jax.experimental.pallas import tpu as pltpu
from jax.sharding import PartitionSpec as P

AB = 64
FB = 64
OB = 128
OWN_CAP = 8
CAP = 2
NY = 4
NZH = 2
NZL = 8
NXC = 8
GROUP = 4
MESH = pl.DeviceIdType.MESH
TOP = 32767.0
TINY = 1e-30


def coded(values):
    top = jnp.maximum(jnp.max(jnp.max(jnp.abs(values), axis=0), axis=0, keepdims=True), TINY)
    whole = jnp.round(values * (TOP / top)[None])
    return whole.astype(jnp.int32).astype(jnp.int16), top * (1.0 / TOP)


def decoded(whole):
    return whole.astype(jnp.int32).astype(jnp.float32)


def exchange_kernel(
    table_ref, occ_of_ref, index_ref, x_ref, res_ref, target_ref, out_ref,
    occ_all, wide, res, acc, qy, sy, ry, rsy, qa, sa, ra, rsa, rb, rsb, flat, final,
    send_own, recv_own, send_z, recv_z, send_fw, recv_fw, local_sem,
    send_y, recv_y, send_a, recv_a, send_b, recv_b,
):
    fit = lax.axis_index("fit")
    ao = lax.axis_index("ao")
    y, zh = fit // NZH, fit % NZH
    zl, xc = ao // NXC, ao % NXC
    fits = NY * NZH
    partner = y * NZH + (1 - zh)
    blocks = x_ref.shape[0] // FB
    occs = out_ref.shape[2] // OB
    tiles = res_ref.shape[0]
    per_step = tiles // fits
    half = wide.shape[1] // 2

    def at_y(d):
        return (((y + d) % NY) * NZH + zh, ao)

    def at_z(i, other):
        return (y * NZH + other, ((zl + i) % NZL) * NXC + xc)

    def at_x(d):
        return (fit, zl * NXC + (xc + d) % NXC)

    fill = pltpu.make_async_copy(res_ref, res.at[pl.ds(0, tiles)], local_sem)
    fill.start()
    barrier = pltpu.get_barrier_semaphore()
    pl.semaphore_signal(barrier, inc=1, device_id=(partner, ao), device_id_type=MESH)
    for d in range(1, NY):
        pl.semaphore_signal(barrier, inc=1, device_id=at_y(d), device_id_type=MESH)
    for i in range(1, NZL):
        for other in range(NZH):
            pl.semaphore_signal(barrier, inc=1, device_id=at_z(i, other), device_id_type=MESH)
    for d in range(1, NXC):
        pl.semaphore_signal(barrier, inc=1, device_id=at_x(d), device_id_type=MESH)
    pl.semaphore_wait(barrier, NY + (NZL - 1) * NZH + NXC - 1)

    across = []
    for j in range(blocks):
        copy = pltpu.make_async_remote_copy(
            src_ref=x_ref.at[pl.ds(j * FB, FB)],
            dst_ref=occ_all.at[fit, pl.ds(j * FB, FB)],
            send_sem=send_z.at[j],
            recv_sem=recv_z.at[j],
            device_id=(partner, ao),
            device_id_type=MESH,
        )
        copy.start()
        across.append(copy)
    own = []
    for d in range(1, NY):
        copy = pltpu.make_async_remote_copy(
            src_ref=x_ref,
            dst_ref=occ_all.at[fit],
            send_sem=send_own.at[d - 1],
            recv_sem=recv_own.at[d - 1],
            device_id=at_y(d),
            device_id_type=MESH,
        )
        copy.start()
        own.append(copy)

    wide[...] = jnp.zeros_like(wide)
    res[tiles] = jnp.zeros(res.shape[1:], res.dtype)
    occ_all[fit] = x_ref[...]

    def spread(part):
        def one(i, _):
            source = (fit - (2 * i + part) + fits) % fits
            for j in range(blocks):
                at = pl.multiple_of(part * half + (i * blocks + j) * 2 * FB, 2 * FB)
                for o in range(occs):
                    piece = occ_all[source, j * FB : (j + 1) * FB, o * OB : (o + 1) * OB]
                    wide[o, pl.ds(at, FB), :OB] = piece
                    wide[o, pl.ds(at + FB, FB), OB:] = piece
            return 0

        lax.fori_loop(0, fits // 2, one, 0)

    def multiply(part):
        def one(g, _):
            rows = []
            for u in range(GROUP):
                rows.append(jnp.concatenate(
                    [
                        res[table_ref[j * fits + 2 * i + part, g * GROUP + u]]
                        for i in range(fits // 2)
                        for j in range(blocks)
                    ],
                    axis=1,
                ))
            weights = wide[occ_of_ref[g], part * half : (part + 1) * half, :]
            value = jnp.dot(jnp.concatenate(rows, axis=0), weights, preferred_element_type=jnp.float32)
            height = AB // 2
            for u in range(GROUP):
                parts = []
                for k in range(NY):
                    at = u * height + k * 8
                    parts += [value[at : at + 8, :OB], value[at : at + 8, OB:]]
                tile = jnp.concatenate(parts, axis=0)
                if part == 0:
                    acc[g * GROUP + u] = tile
                else:
                    acc[g * GROUP + u] += tile
            return 0

        lax.fori_loop(0, acc.shape[0] // GROUP, one, 0)

    for copy in own:
        copy.wait_recv()
    spread(0)
    fill.wait()

    forward = []
    multiply(0)
    for j in range(blocks):
        across[j].wait_recv()
        for d in range(1, NY):
            copy = pltpu.make_async_remote_copy(
                src_ref=occ_all.at[partner, pl.ds(j * FB, FB)],
                dst_ref=occ_all.at[partner, pl.ds(j * FB, FB)],
                send_sem=send_fw.at[j, d - 1],
                recv_sem=recv_fw.at[j, d - 1],
                device_id=at_y(d),
                device_id_type=MESH,
            )
            copy.start()
            forward.append(copy)
    for copy in forward:
        copy.wait_recv()
    spread(1)
    multiply(1)

    per_block = NXC * CAP
    groups = per_block // 8

    def copies_y(i):
        made = []
        for d in range(1, NY):
            for n, (src, dst) in enumerate(((qy, ry), (sy, rsy))):
                made.append(pltpu.make_async_remote_copy(
                    src_ref=src.at[i, d - 1],
                    dst_ref=dst.at[i, d - 1],
                    send_sem=send_y.at[i, n, d - 1],
                    recv_sem=recv_y.at[i, n, d - 1],
                    device_id=at_y(d),
                    device_id_type=MESH,
                ))
        return made

    def copies_a(i, other):
        return [
            pltpu.make_async_remote_copy(
                src_ref=src.at[i, other],
                dst_ref=dst.at[i, zh],
                send_sem=send_a.at[i, n, other],
                recv_sem=recv_a.at[i, n, zh],
                device_id=at_z(i, other),
                device_id_type=MESH,
            )
            for n, (src, dst) in enumerate(((qa, ra), (sa, rsa)))
        ]

    def code(i):
        first = ((zl + i) % NZL) * per_block
        for d in range(1, NY):
            at = pl.multiple_of(((y + d) % NY) * 16, 16)
            for g in range(groups):
                values = jnp.concatenate(
                    [acc[index_ref[first + g * 8 + n], pl.ds(at, 16), :][None] for n in range(8)], axis=0
                )
                whole, scale = coded(values)
                qy[i, d - 1, g * 8 : g * 8 + 8] = whole
                sy[i, d - 1, g] = scale
        for copy in copies_y(i):
            copy.start()

    lower = lax.broadcasted_iota(jnp.int32, (8, OB), 0) < 4
    mine = pl.multiple_of(y * 16, 16)

    def collect(i):
        first = ((zl + i) % NZL) * per_block
        for copy in copies_y(i):
            copy.wait_recv()
        firsts, seconds = [], []
        for other in range(NXC):
            halves = ([], [])
            for rank in range(CAP):
                n = other * CAP + rank
                tile = acc[index_ref[first + n], pl.ds(mine, 16), :]
                for d in range(NY - 1):
                    tile = tile + decoded(ry[i, d, n]) * rsy[i, d, n // 8]
                a, b = tile[:8], tile[8:]
                halves[0].append(jnp.where(lower, a, pltpu.roll(b, 4, 0)))
                halves[1].append(jnp.where(lower, pltpu.roll(a, 4, 0), b))
            firsts.append(jnp.concatenate(halves[0], axis=0)[None])
            seconds.append(jnp.concatenate(halves[1], axis=0)[None])
        for k, values in enumerate((firsts, seconds)):
            whole, scale = coded(jnp.concatenate(values, axis=0))
            qa[i, k] = whole
            sa[i, k] = scale

    def send_on(i):
        for other in range(NZH):
            for copy in copies_a(i, other):
                copy.start()

    code(0)
    code(1)
    collect(0)
    first_a = copies_a(0, 1 - zh)
    for copy in first_a:
        copy.start()
    ra[0, zh] = qa[0, zh]
    rsa[0, zh] = sa[0, zh]

    def turn(i, _):
        code(i + 1)
        collect(i)
        send_on(i)
        return 0

    lax.fori_loop(1, NZL - 1, turn, 0)
    collect(NZL - 1)
    send_on(NZL - 1)

    def arrived(i, source):
        for n, dst in enumerate((ra, rsa)):
            pltpu.make_async_remote_copy(
                src_ref=dst.at[i, source],
                dst_ref=dst.at[i, source],
                send_sem=send_a.at[i, n, source],
                recv_sem=recv_a.at[i, n, source],
                device_id=at_z(i, source),
                device_id_type=MESH,
            ).wait_recv()

    def later(i, _):
        for source in range(NZH):
            arrived(i, source)
        return 0

    copies_b = []
    parts = 2
    span = NZL // parts
    for part in range(parts):
        if part == 0:
            arrived(0, 1 - zh)
        lax.fori_loop(max(part * span, 1), (part + 1) * span, later, 0)
        here = pl.ds(part * span, span)
        for d in range(1, NXC):
            other = (xc + d) % NXC
            for n, (src, dst) in enumerate((
                (ra.at[here, :, other], rb.at[xc, here]),
                (rsa.at[here], rsb.at[xc, here]),
            )):
                copy = pltpu.make_async_remote_copy(
                    src_ref=src,
                    dst_ref=dst,
                    send_sem=send_b.at[part, n, d - 1],
                    recv_sem=recv_b.at[part, n, d - 1],
                    device_id=at_x(d),
                    device_id_type=MESH,
                )
                copy.start()
                copies_b.append(copy)
    for i in range(NZL):
        rb[xc, i] = ra[i, :, xc]
    rsb[xc] = rsa[...]
    for copy in copies_b:
        copy.wait_recv()

    def expand(source, _):
        for i in range(NZL):
            for k in range(NZH):
                value = decoded(rb[source, i, k]) * rsb[source, i, k]
                flat[pl.ds(pl.multiple_of(((source * NZL + i) * NZH + k) * 16, 16), 16), :] = value
        return 0

    lax.fori_loop(0, NXC, expand, 0)
    entries = NXC * NZL * NZH * CAP
    names = lax.broadcasted_iota(jnp.int32, (occs * OWN_CAP, entries), 0)
    select = (names == target_ref[...]).astype(jnp.float32)
    for m in range(8):
        part = jnp.dot(
            select, flat[pl.ds(m, entries, stride=8), :],
            precision=lax.Precision.HIGHEST, preferred_element_type=jnp.float32,
        )
        row = 2 * (m % 4) + m // 4
        for o in range(occs):
            final[o, pl.ds(row, OWN_CAP, stride=8), :] = part[o * OWN_CAP : (o + 1) * OWN_CAP]
    for o in range(occs):
        out_ref[:, :, o * OB : (o + 1) * OB] = final[o].reshape(OWN_CAP, 8, OB).astype(out_ref.dtype)

    for copy in across + own + forward + copies_b + first_a:
        copy.wait_send()

    def sent_y(i, _):
        for copy in copies_y(i):
            copy.wait_send()
        return 0

    def sent_a(i, _):
        for other in range(NZH):
            for copy in copies_a(i, other):
                copy.wait_send()
        return 0

    lax.fori_loop(0, NZL, sent_y, 0)
    lax.fori_loop(1, NZL, sent_a, 0)


def exchange(table, occ_of, index, occ, rows, target):
    i16, f32, bf16 = jnp.int16, jnp.float32, jnp.bfloat16
    blocks, occs = occ.shape[0] // FB, occ.shape[1] // OB
    fits = NY * NZH
    slots = table.shape[1]
    dma = pltpu.SemaphoreType.DMA
    smem, vmem = pl.BlockSpec(memory_space=pltpu.SMEM), pl.BlockSpec(memory_space=pltpu.VMEM)
    return pl.pallas_call(
        exchange_kernel,
        out_shape=jax.ShapeDtypeStruct((OWN_CAP, AB // fits, occ.shape[1]), bf16),
        in_specs=[smem, smem, smem, vmem, pl.BlockSpec(memory_space=pl.ANY), vmem],
        out_specs=vmem,
        scratch_shapes=[
            pltpu.VMEM((fits,) + occ.shape, bf16),
            pltpu.VMEM((occs, fits * blocks * 2 * FB, 2 * OB), bf16),
            pltpu.VMEM((rows.shape[0] + 1,) + rows.shape[1:], bf16),
            pltpu.VMEM((slots, AB, OB), f32),
            pltpu.VMEM((NZL, NY - 1, NXC * CAP, 16, OB), i16),
            pltpu.VMEM((NZL, NY - 1, NXC * CAP // 8, 1, OB), f32),
            pltpu.VMEM((NZL, NY - 1, NXC * CAP, 16, OB), i16),
            pltpu.VMEM((NZL, NY - 1, NXC * CAP // 8, 1, OB), f32),
            pltpu.VMEM((NZL, NZH, NXC, 16, OB), i16),
            pltpu.VMEM((NZL, NZH, 1, OB), f32),
            pltpu.VMEM((NZL, NZH, NXC, 16, OB), i16),
            pltpu.VMEM((NZL, NZH, 1, OB), f32),
            pltpu.VMEM((NXC, NZL, NZH, 16, OB), i16),
            pltpu.VMEM((NXC, NZL, NZH, 1, OB), f32),
            pltpu.VMEM((NXC * NZL * NZH * 16, OB), f32),
            pltpu.VMEM((occs, OWN_CAP * 8, OB), f32),
            dma((NY - 1,)), dma((NY - 1,)), dma((blocks,)), dma((blocks,)),
            dma((blocks, NY - 1)), dma((blocks, NY - 1)), dma,
            dma((NZL, 2, NY - 1)), dma((NZL, 2, NY - 1)),
            dma((NZL, 2, NZH)), dma((NZL, 2, NZH)),
            dma((2, 2, NXC - 1)), dma((2, 2, NXC - 1)),
        ],
        compiler_params=pltpu.CompilerParams(collective_id=0, has_side_effects=True, vmem_limit_bytes=48 << 20),
        name="exchange",
    )(table, occ_of, index, occ, rows, target)


def before(n):
    at = jnp.arange(n)
    return (at[:, None] < at[None, :]).astype(jnp.float32)


def earlier_like(values):
    at = jnp.arange(values.shape[0])
    same = (values[:, None] == values[None, :]) & (at[None, :] < at[:, None])
    return jnp.sum(same.astype(jnp.int32), axis=1)


def plan(codes, occs, tiles_slots):
    occ_of = codes % occs
    kinds = jnp.arange(occs)
    counts = jnp.sum((occ_of[None, :] == kinds[:, None]).astype(jnp.int32), axis=1)
    padded = (counts + GROUP - 1) // GROUP * GROUP
    starts = jnp.sum(jnp.where(kinds[None, :] < kinds[:, None], padded[None, :], 0), axis=1)
    slot = earlier_like(occ_of) + jnp.sum(jnp.where(occ_of[:, None] == kinds[None, :], starts[None, :], 0), axis=1)
    firsts = jnp.arange(tiles_slots // GROUP) * GROUP
    group_occ = jnp.sum((firsts[:, None] >= starts[None, :]).astype(jnp.int32), axis=1) - 1
    return slot, group_occ


def pair_table(row_tiles, row_pairs, live_rows, slot, slots, none):
    blocks, steps, width = row_pairs.shape
    per_step = none // steps
    usable = (row_pairs >= 0) & (jnp.arange(width) < live_rows[:, None])[None]
    at = jnp.sum(jnp.where(row_tiles[:, :, None] == jnp.arange(slot.shape[0]), slot, 0), axis=2)
    value = jnp.where(usable, row_pairs + (jnp.arange(steps) * per_step)[None, :, None] - none, 0)
    hit = at[None, :, None, :] == jnp.arange(slots)[None, None, :, None]
    return (jnp.sum(jnp.where(hit, value[:, :, None, :], 0), axis=3) + none).reshape(blocks * steps, slots)


def routing(tile_list, codes, owner_slot, slot, column, occs):
    blocks = owner_slot.shape[0]
    tiles = codes.shape[0]
    ao_count = tile_list.shape[0]
    numbers = jnp.arange(blocks)
    owned_at = jnp.sum(jnp.where((codes // occs)[:, None] == numbers, owner_slot, 0), axis=1)
    owners = owned_at // OWN_CAP
    places = owners * CAP + earlier_like(owners)
    index = jnp.sum(jnp.where(places[None, :] == jnp.arange(ao_count * CAP)[:, None], slot[None, :], 0), axis=1)

    mine = column * OWN_CAP + jnp.arange(OWN_CAP)
    held = jnp.sum(jnp.where(owner_slot[None, :] == mine[:, None], numbers[None, :] + 1, 0), axis=1) - 1
    names = tile_list // occs
    place = jnp.sum(
        jnp.where(names[:, :, None] == held[None, None, :], jnp.arange(OWN_CAP) + 1, 0), axis=2
    ) - 1
    owned = place >= 0
    goal = (tile_list % occs) * OWN_CAP + place
    rank = jnp.dot(owned.astype(jnp.float32), before(tiles)).astype(jnp.int32)
    target = jnp.stack(
        [jnp.sum(jnp.where(owned & (rank == r), goal + 1, 0), axis=1) - 1 for r in range(CAP)], axis=1
    )
    target = target.reshape(NZL, NXC, CAP)
    sources = (column // NXC - jnp.arange(NZL)) % NZL
    turned = jnp.sum(
        jnp.where((sources[:, None] == jnp.arange(NZL)[None, :])[:, :, None, None], target[None], 0), axis=1
    )
    turned = jnp.broadcast_to(turned.transpose(1, 0, 2)[:, :, None], (NXC, NZL, NZH, CAP))
    return index, turned.reshape(1, -1)


def shards(occ_blocks, resident, row_tiles, row_pairs, live_rows, tile_list, owner_slot):
    column = lax.axis_index("ao")
    occs = occ_blocks.shape[1] // OB
    codes = lax.dynamic_index_in_dim(tile_list, column, 0, keepdims=False)
    slots = codes.shape[0] + occs * GROUP
    slot, group_occ = plan(codes, occs, slots)
    table = pair_table(row_tiles[0], row_pairs[:, 0], live_rows[0], slot, slots, resident.shape[0])
    index, target = routing(tile_list, codes, owner_slot, slot, column, occs)
    rows = resident.reshape(resident.shape[0], AB // 2, 2 * FB)
    return exchange(table, group_occ, index, occ_blocks, rows, target)


def solution(mesh):
    return jax.shard_map(
        shards,
        mesh=mesh,
        in_specs=(
            P(("fit", "ao"), None),
            P(("fit", "ao"), None),
            P(("fit", "ao"), None, None),
            P(None, ("fit", "ao"), None, None),
            P(("fit", "ao"), None),
            P(),
            P(),
        ),
        out_specs=P("ao", "fit", None),
        check_vma=False,
    )
```

time: 939 us -> 112 us (0.12)
  starting transfers between devices: 350 us -> 0 us
  waiting for transfers between devices: 308 us -> 0 us
  local copies, waits for them, and re-layouts: 160 us -> 3.2 us
  Pallas kernels: 0 us -> 98.3 us
  other arithmetic: 70.9 us -> 8.42 us
  matrix products: 22.4 us -> 1.01 us
  between operations: 14.4 us -> 0.16 us
    ppermute x7 -> x0, starting transfers between devices: 285 us -> none  [from_behind(): return lax.ppermute(block, axis, route)]
    all_to_all x1 -> x0, waiting for transfers between devices: 162 us -> none  [shards(): lax.all_to_all(outgoing, 'ao', split_axis=0, concat_axis=0, tiled=True)]
    reduce_scatter x1 -> x0, waiting for transfers between devices: 109 us -> none  [shards(): result = lax.psum_scatter(summed, 'fit', scatter_dimension=1, tiled=True)]
    pallas_call x0 -> x1, Pallas kernels: none -> 98.3 us  [exchange(): pl.pallas_call(exchange_kernel, out_shape=jax.ShapeDtypeStruct((OWN_CAP,...]
    gather x34 -> x0, local copies, waits for them, and re-layouts: 88.5 us -> none  [the longest x2 38.6 us: routing(): slot_ids = owner_slot[tile_list // occ_count]]
    all_to_all x1 -> x0, starting transfers between devices: 65.7 us -> none  [shards(): lax.all_to_all(outgoing, 'ao', split_axis=0, concat_axis=0, tiled=True)]
    scatter-add x9 -> x0, other arithmetic: 52.7 us -> none  [the longest x8 39.2 us: one_block(): return running.at[tile_ids].add(product)]
    scatter x2 -> x0, local copies, waits for them, and re-layouts: 37.6 us -> none  [the longest x1 23 us: unpack(): target_at.at[position.reshape(-1)].set(targets.reshape(-1), mode='drop')]
  transfers between devices with their start and end apart: 9 -> 0, of which waited for: 6 -> 0; matrix products, arithmetic and copies ran while one was open for 5% -> 0% of each run, Pallas kernels for 0% -> 0%
where the time goes in v2:
time: 112 us; the launch traced here: 111 us
  Pallas kernels  98.3 us (88%)
  other arithmetic  8.42 us (8%)
  local copies, waits for them, and re-layouts  3.2 us (3%)
    pallas_call x1, Pallas kernels, exchange(): pl.pallas_call(exchange_kernel, out_shape=jax.ShapeDtypeStruct((OWN_CAP,...  98.3 us
    unnamed x4, local copies, waits for them, and re-layouts  2.75 us

profile of v2, /device:TPU:1, one launch (start us, length us, event | category | flops | bytes accessed | tf_op | source)
XLA Modules:
  0.0 111.1 jit_solution(2378603244131600934)
XLA Ops:
  0.0 0.7 fusion.10
  0.7 0.1 convert_reduce_fusion.3
  0.9 0.1 select_reduce_fusion.10
  1.0 0.1 iota_compare_fusion.7
  1.1 0.1 convert_reduce_fusion.2
  1.2 0.7 and_select_fusion.2
  1.9 0.9 select_reduce_fusion.3
  2.7 0.1 select_reduce_fusion.9
  2.8 0.2 convert_reduce_fusion.1
  3.0 0.2 convert_reduce_fusion
  3.2 0.1 select_reduce_fusion.5.index_ref
  3.3 0.7 iota_compare_fusion.8
  4.1 0.9 select_reduce_fusion.8
  4.9 1.0 select_reduce_fusion.1
  6.0 0.8 fusion.8
  6.8 0.8 add_select_fusion.1
  7.5 0.2 select_reduce_fusion.2
  7.7 1.0 select_reduce_fusion.7
  8.7 0.1 sub.78
  8.8 0.1 sub.76
  8.9 0.1 select_reduce_fusion.4
  9.0 0.1 copy.10
  9.2 0.1 reshape.252.target_ref
  9.3 0.2 iota_compare_fusion
  9.5 0.5 select_reduce_fusion
  10.0 0.0 copy-start
  10.0 2.1 %copy.11 = bf16[32,8,32,128]{3,2,1,0:T(8,128)(2,1)S(1)} copy(bf16[32,8,32,128]{3,1,2,0:T(8,128)(2,1)} %bitcast.35) | data formatting | bytes 4194304
  12.1 0.0 copy-done
  12.2 98.3 %exchange.1 = bf16[8,8,512]{2,1,0:T(8,128)(2,1)S(1)} custom-call(s32[24,112]{1,0:T(8,128)S(1)} %add_bitcast_fusion.table_ref, s32[28]{0:T(128)S(1)} %broadcast_add_fusion.3.occ_of_ref, s32[128]{0:T(128)S(1)} %select_reduce_fusion.5.index_ref, bf16[192,512]{1,0:T(8,128)(2,1)S(1)} %copy-done, bf16[256,32,128]{2,1,0:T(8,128)(2,1)S(1)} %bitcast.34, ...), custom_call_target="tpu_custom_call" | custom-call | tf_op jit(solution)/shard_map/exchange/pallas_call | solution.py:357
  110.5 0.6 copy.13
  (17 shorter events, 0.1 us)
Async XLA Ops:
  10.0 2.1 %copy-start = (bf16[192,512]{1,0:T(8,128)(2,1)S(1)}, bf16[192,512]{1,0:T(8,128)(2,1)}, u32[]{:S(2)}) copy-start(bf16[192,512]{1,0:T(8,128)(2,1)} %x_ref.1) | copy-start | bytes 589828

commit v3 on v2

--- a/solution.py
+++ b/solution.py
@@ -17,9 +17,15 @@
 NZL = 8
 NXC = 8
 GROUP = 4
+PARTS = 4
 MESH = pl.DeviceIdType.MESH
 TOP = 32767.0
 TINY = 1e-30
+
+
+def offset(k):
+    odd = k % 2
+    return odd * ((k + 1) // 2) + (1 - odd) * ((NZL - k // 2) % NZL)
 
 
 def coded(values):
@@ -34,7 +40,7 @@
 
 def exchange_kernel(
     table_ref, occ_of_ref, index_ref, x_ref, res_ref, target_ref, out_ref,
-    occ_all, wide, res, acc, qy, sy, ry, rsy, qa, sa, ra, rsa, rb, rsb, flat, final,
+    occ_all, wide, res, acc, qy, sy, ry, rsy, qa, sa, ra, rsa, rb, rsb, flat, summed, final,
     send_own, recv_own, send_z, recv_z, send_fw, recv_fw, local_sem,
     send_y, recv_y, send_a, recv_a, send_b, recv_b,
 ):
@@ -54,7 +60,7 @@
         return (((y + d) % NY) * NZH + zh, ao)
 
     def at_z(i, other):
-        return (y * NZH + other, ((zl + i) % NZL) * NXC + xc)
+        return (y * NZH + other, ((zl + offset(i)) % NZL) * NXC + xc)
 
     def at_x(d):
         return (fit, zl * NXC + (xc + d) % NXC)
@@ -101,11 +107,14 @@
     res[tiles] = jnp.zeros(res.shape[1:], res.dtype)
     occ_all[fit] = x_ref[...]
 
-    def spread(part):
+    def place(part, i, j):
+        return (i * blocks + j if part == 0 else (fits // 2) * (blocks + j) + i) * 2 * FB
+
+    def spread(part, wanted):
         def one(i, _):
             source = (fit - (2 * i + part) + fits) % fits
-            for j in range(blocks):
-                at = pl.multiple_of(part * half + (i * blocks + j) * 2 * FB, 2 * FB)
+            for j in wanted:
+                at = pl.multiple_of(place(part, i, j), 2 * FB)
                 for o in range(occs):
                     piece = occ_all[source, j * FB : (j + 1) * FB, o * OB : (o + 1) * OB]
                     wide[o, pl.ds(at, FB), :OB] = piece
@@ -114,19 +123,18 @@
 
         lax.fori_loop(0, fits // 2, one, 0)
 
-    def multiply(part):
+    def multiply(part, wanted, first, last):
+        order = [(place(part, i, j), i, j) for i in range(fits // 2) for j in wanted]
+        order.sort()
+        start = order[0][0]
+
         def one(g, _):
             rows = []
             for u in range(GROUP):
                 rows.append(jnp.concatenate(
-                    [
-                        res[table_ref[j * fits + 2 * i + part, g * GROUP + u]]
-                        for i in range(fits // 2)
-                        for j in range(blocks)
-                    ],
-                    axis=1,
+                    [res[table_ref[j * fits + 2 * i + part, g * GROUP + u]] for _, i, j in order], axis=1
                 ))
-            weights = wide[occ_of_ref[g], part * half : (part + 1) * half, :]
+            weights = wide[occ_of_ref[g], start : start + len(order) * 2 * FB, :]
             value = jnp.dot(jnp.concatenate(rows, axis=0), weights, preferred_element_type=jnp.float32)
             height = AB // 2
             for u in range(GROUP):
@@ -141,17 +149,11 @@
                     acc[g * GROUP + u] += tile
             return 0
 
-        lax.fori_loop(0, acc.shape[0] // GROUP, one, 0)
-
-    for copy in own:
-        copy.wait_recv()
-    spread(0)
-    fill.wait()
-
-    forward = []
-    multiply(0)
-    for j in range(blocks):
+        lax.fori_loop(first, last, one, 0)
+
+    def pass_on(j):
         across[j].wait_recv()
+        made = []
         for d in range(1, NY):
             copy = pltpu.make_async_remote_copy(
                 src_ref=occ_all.at[partner, pl.ds(j * FB, FB)],
@@ -162,11 +164,25 @@
                 device_id_type=MESH,
             )
             copy.start()
-            forward.append(copy)
-    for copy in forward:
+            made.append(copy)
+        return made
+
+    for copy in own:
         copy.wait_recv()
-    spread(1)
-    multiply(1)
+    spread(0, range(blocks))
+    fill.wait()
+    all_groups = acc.shape[0] // GROUP
+    multiply(0, range(blocks), 0, all_groups // 2)
+    forward = [pass_on(0)]
+    multiply(0, range(blocks), all_groups // 2, all_groups)
+    for j in range(blocks):
+        for copy in forward[j]:
+            copy.wait_recv()
+        spread(1, [j])
+        multiply(1, [j], 0, all_groups)
+        if j + 1 < blocks:
+            forward.append(pass_on(j + 1))
+    forward = [copy for made in forward for copy in made]
 
     per_block = NXC * CAP
     groups = per_block // 8
@@ -199,7 +215,7 @@
         ]
 
     def code(i):
-        first = ((zl + i) % NZL) * per_block
+        first = ((zl + offset(i)) % NZL) * per_block
         for d in range(1, NY):
             at = pl.multiple_of(((y + d) % NY) * 16, 16)
             for g in range(groups):
@@ -216,7 +232,7 @@
     mine = pl.multiple_of(y * 16, 16)
 
     def collect(i):
-        first = ((zl + i) % NZL) * per_block
+        first = ((zl + offset(i)) % NZL) * per_block
         for copy in copies_y(i):
             copy.wait_recv()
         firsts, seconds = [], []
@@ -277,19 +293,22 @@
             arrived(i, source)
         return 0
 
+    span = NZL // PARTS
+    entries = NXC * span * NZH * CAP
+    names = lax.broadcasted_iota(jnp.int32, (occs * OWN_CAP, entries), 0)
     copies_b = []
-    parts = 2
-    span = NZL // parts
-    for part in range(parts):
+
+    def send_x(part):
         if part == 0:
             arrived(0, 1 - zh)
         lax.fori_loop(max(part * span, 1), (part + 1) * span, later, 0)
         here = pl.ds(part * span, span)
+        made = []
         for d in range(1, NXC):
             other = (xc + d) % NXC
             for n, (src, dst) in enumerate((
-                (ra.at[here, :, other], rb.at[xc, here]),
-                (rsa.at[here], rsb.at[xc, here]),
+                (ra.at[here, :, other], rb.at[part, xc]),
+                (rsa.at[here], rsb.at[part, xc]),
             )):
                 copy = pltpu.make_async_remote_copy(
                     src_ref=src,
@@ -300,32 +319,45 @@
                     device_id_type=MESH,
                 )
                 copy.start()
-                copies_b.append(copy)
-    for i in range(NZL):
-        rb[xc, i] = ra[i, :, xc]
-    rsb[xc] = rsa[...]
-    for copy in copies_b:
-        copy.wait_recv()
-
-    def expand(source, _):
-        for i in range(NZL):
-            for k in range(NZH):
-                value = decoded(rb[source, i, k]) * rsb[source, i, k]
-                flat[pl.ds(pl.multiple_of(((source * NZL + i) * NZH + k) * 16, 16), 16), :] = value
-        return 0
-
-    lax.fori_loop(0, NXC, expand, 0)
-    entries = NXC * NZL * NZH * CAP
-    names = lax.broadcasted_iota(jnp.int32, (occs * OWN_CAP, entries), 0)
-    select = (names == target_ref[...]).astype(jnp.float32)
-    for m in range(8):
-        part = jnp.dot(
-            select, flat[pl.ds(m, entries, stride=8), :],
-            precision=lax.Precision.HIGHEST, preferred_element_type=jnp.float32,
-        )
-        row = 2 * (m % 4) + m // 4
-        for o in range(occs):
-            final[o, pl.ds(row, OWN_CAP, stride=8), :] = part[o * OWN_CAP : (o + 1) * OWN_CAP]
+                made.append(copy)
+        for i in range(span):
+            rb[part, xc, i] = ra[part * span + i, :, xc]
+            rsb[part, xc, i] = rsa[part * span + i]
+        copies_b.append(made)
+
+    def add_up(part):
+        for copy in copies_b[part]:
+            copy.wait_recv()
+
+        def expand(source, _):
+            for i in range(span):
+                for k in range(NZH):
+                    value = decoded(rb[part, source, i, k]) * rsb[part, source, i, k]
+                    flat[part, pl.ds(pl.multiple_of(((source * span + i) * NZH + k) * 16, 16), 16), :] = value
+            return 0
+
+        lax.fori_loop(0, NXC, expand, 0)
+        select = (names == target_ref[part : part + 1, :]).astype(jnp.float32)
+        for m in range(8):
+            total = jnp.dot(
+                select, flat[part, pl.ds(m, entries, stride=8), :],
+                precision=lax.Precision.HIGHEST, preferred_element_type=jnp.float32,
+            )
+            if part:
+                total += summed[m]
+            if part + 1 < PARTS:
+                summed[m] = total
+                continue
+            row = 2 * (m % 4) + m // 4
+            for o in range(occs):
+                final[o, pl.ds(row, OWN_CAP, stride=8), :] = total[o * OWN_CAP : (o + 1) * OWN_CAP]
+
+    for part in range(PARTS):
+        send_x(part)
+        if part:
+            add_up(part - 1)
+    add_up(PARTS - 1)
+    copies_b = [copy for made in copies_b for copy in made]
     for o in range(occs):
         out_ref[:, :, o * OB : (o + 1) * OB] = final[o].reshape(OWN_CAP, 8, OB).astype(out_ref.dtype)
 
@@ -372,15 +404,16 @@
             pltpu.VMEM((NZL, NZH, 1, OB), f32),
             pltpu.VMEM((NZL, NZH, NXC, 16, OB), i16),
             pltpu.VMEM((NZL, NZH, 1, OB), f32),
-            pltpu.VMEM((NXC, NZL, NZH, 16, OB), i16),
-            pltpu.VMEM((NXC, NZL, NZH, 1, OB), f32),
-            pltpu.VMEM((NXC * NZL * NZH * 16, OB), f32),
+            pltpu.VMEM((PARTS, NXC, NZL // PARTS, NZH, 16, OB), i16),
+            pltpu.VMEM((PARTS, NXC, NZL // PARTS, NZH, 1, OB), f32),
+            pltpu.VMEM((PARTS, NXC * NZL // PARTS * NZH * 16, OB), f32),
+            pltpu.VMEM((8, occs * OWN_CAP, OB), f32),
             pltpu.VMEM((occs, OWN_CAP * 8, OB), f32),
             dma((NY - 1,)), dma((NY - 1,)), dma((blocks,)), dma((blocks,)),
             dma((blocks, NY - 1)), dma((blocks, NY - 1)), dma,
             dma((NZL, 2, NY - 1)), dma((NZL, 2, NY - 1)),
             dma((NZL, 2, NZH)), dma((NZL, 2, NZH)),
-            dma((2, 2, NXC - 1)), dma((2, 2, NXC - 1)),
+            dma((PARTS, 2, NXC - 1)), dma((PARTS, 2, NXC - 1)),
         ],
         compiler_params=pltpu.CompilerParams(collective_id=0, has_side_effects=True, vmem_limit_bytes=48 << 20),
         name="exchange",
@@ -443,12 +476,13 @@
         [jnp.sum(jnp.where(owned & (rank == r), goal + 1, 0), axis=1) - 1 for r in range(CAP)], axis=1
     )
     target = target.reshape(NZL, NXC, CAP)
-    sources = (column // NXC - jnp.arange(NZL)) % NZL
+    sources = (column // NXC - offset(jnp.arange(NZL))) % NZL
     turned = jnp.sum(
         jnp.where((sources[:, None] == jnp.arange(NZL)[None, :])[:, :, None, None], target[None], 0), axis=1
     )
-    turned = jnp.broadcast_to(turned.transpose(1, 0, 2)[:, :, None], (NXC, NZL, NZH, CAP))
-    return index, turned.reshape(1, -1)
+    turned = turned.reshape(PARTS, NZL // PARTS, NXC, CAP).transpose(0, 2, 1, 3)
+    turned = jnp.broadcast_to(turned[:, :, :, None], (PARTS, NXC, NZL // PARTS, NZH, CAP))
+    return index, turned.reshape(PARTS, -1)
 
 
 def shards(occ_blocks, resident, row_tiles, row_pairs, live_rows, tile_list, owner_slot):

time: 112 us -> 117 us (1.045)
  Pallas kernels: 98.3 us -> 104 us
    pallas_call x1, Pallas kernels: 98.3 us -> 104 us  [exchange(): pl.pallas_call(exchange_kernel, out_shape=jax.ShapeDtypeStruct((OWN_CAP,...]
where the time goes in v3:
time: 117 us; the launch traced here: 116 us
  Pallas kernels  104 us (89%)
  other arithmetic  8.43 us (7%)
  local copies, waits for them, and re-layouts  3.09 us (3%)
    pallas_call x1, Pallas kernels, exchange(): pl.pallas_call(exchange_kernel, out_shape=jax.ShapeDtypeStruct((OWN_CAP,...  104 us
    unnamed x4, local copies, waits for them, and re-layouts  2.75 us

profile of v3, /device:TPU:1, one launch (start us, length us, event | category | flops | bytes accessed | tf_op | source)
XLA Modules:
  0.0 116.2 jit_solution(9636977653630026392)
XLA Ops:
  0.0 0.7 fusion.13
  0.7 0.1 convert_reduce_fusion.3
  0.9 0.1 select_reduce_fusion.10
  1.0 0.1 iota_compare_fusion.7
  1.1 0.1 convert_reduce_fusion.2
  1.2 0.7 and_select_fusion.6
  1.9 0.9 select_reduce_fusion.3
  2.7 0.1 select_reduce_fusion.9
  2.8 0.2 convert_reduce_fusion.1
  3.0 0.2 convert_reduce_fusion
  3.2 0.1 select_reduce_fusion.5.index_ref
  3.3 0.7 iota_compare_fusion.8
  4.1 0.9 select_reduce_fusion.8
  4.9 1.0 select_reduce_fusion.1
  6.0 0.8 fusion.8
  6.8 0.8 add_select_fusion.1
  7.6 0.2 select_reduce_fusion.2
  7.7 1.0 select_reduce_fusion.7
  8.7 0.1 sub.103
  8.8 0.1 sub.101
  8.9 0.1 select_reduce_fusion.4
  9.0 0.1 copy.14
  9.2 0.1 copy.15.target_ref
  9.2 0.2 iota_compare_fusion
  9.4 0.5 select_reduce_fusion
  9.9 0.0 copy-start
  9.9 2.1 %copy.16 = bf16[32,8,32,128]{3,2,1,0:T(8,128)(2,1)S(1)} copy(bf16[32,8,32,128]{3,1,2,0:T(8,128)(2,1)} %bitcast.38) | data formatting | bytes 4194304
  12.0 0.0 copy-done
  12.1 103.5 %exchange.1 = bf16[8,8,512]{2,1,0:T(8,128)(2,1)S(1)} custom-call(s32[24,112]{1,0:T(8,128)S(1)} %add_bitcast_fusion.table_ref, s32[28]{0:T(128)S(1)} %broadcast_add_fusion.3.occ_of_ref, s32[128]{0:T(128)S(1)} %select_reduce_fusion.5.index_ref, bf16[192,512]{1,0:T(8,128)(2,1)S(1)} %copy-done, bf16[256,32,128]{2,1,0:T(8,128)(2,1)S(1)} %bitcast.37, ...), custom_call_target="tpu_custom_call" | custom-call | tf_op jit(solution)/shard_map/exchange/pallas_call | solution.py:389
  115.6 0.6 copy.18
  (18 shorter events, 0.1 us)
Async XLA Ops:
  9.9 2.1 %copy-start = (bf16[192,512]{1,0:T(8,128)(2,1)S(1)}, bf16[192,512]{1,0:T(8,128)(2,1)}, u32[]{:S(2)}) copy-start(bf16[192,512]{1,0:T(8,128)(2,1)} %x_ref.1) | copy-start | bytes 589828

commit v4 on v3

--- a/solution.py
+++ b/solution.py
@@ -18,6 +18,11 @@
 NXC = 8
 GROUP = 4
 PARTS = 4
+TOGETHER = 4
+TILES = 96
+OCCS = 4
+OCC_BITS = 2
+PAIRS = 32
 MESH = pl.DeviceIdType.MESH
 TOP = 32767.0
 TINY = 1e-30
@@ -39,7 +44,7 @@
 
 
 def exchange_kernel(
-    table_ref, occ_of_ref, index_ref, x_ref, res_ref, target_ref, out_ref,
+    plan_ref, x_ref, res_ref, target_ref, out_ref,
     occ_all, wide, res, acc, qy, sy, ry, rsy, qa, sa, ra, rsa, rb, rsb, flat, summed, final,
     send_own, recv_own, send_z, recv_z, send_fw, recv_fw, local_sem,
     send_y, recv_y, send_a, recv_a, send_b, recv_b,
@@ -128,28 +133,33 @@
         order.sort()
         start = order[0][0]
 
-        def one(g, _):
+        def product(g):
             rows = []
             for u in range(GROUP):
                 rows.append(jnp.concatenate(
-                    [res[table_ref[j * fits + 2 * i + part, g * GROUP + u]] for _, i, j in order], axis=1
+                    [res[plan_ref[j * fits + 2 * i + part, g * GROUP + u]] for _, i, j in order], axis=1
                 ))
-            weights = wide[occ_of_ref[g], start : start + len(order) * 2 * FB, :]
-            value = jnp.dot(jnp.concatenate(rows, axis=0), weights, preferred_element_type=jnp.float32)
+            weights = wide[plan_ref[blocks * fits + 1, g], start : start + len(order) * 2 * FB, :]
+            return jnp.dot(jnp.concatenate(rows, axis=0), weights, preferred_element_type=jnp.float32)
+
+        def one(step, _):
+            values = [product(step * TOGETHER + n) for n in range(TOGETHER)]
             height = AB // 2
-            for u in range(GROUP):
-                parts = []
-                for k in range(NY):
-                    at = u * height + k * 8
-                    parts += [value[at : at + 8, :OB], value[at : at + 8, OB:]]
-                tile = jnp.concatenate(parts, axis=0)
-                if part == 0:
-                    acc[g * GROUP + u] = tile
-                else:
-                    acc[g * GROUP + u] += tile
+            for n, value in enumerate(values):
+                for u in range(GROUP):
+                    parts = []
+                    for k in range(NY):
+                        at = u * height + k * 8
+                        parts += [value[at : at + 8, :OB], value[at : at + 8, OB:]]
+                    tile = jnp.concatenate(parts, axis=0)
+                    slot = (step * TOGETHER + n) * GROUP + u
+                    if part == 0:
+                        acc[slot] = tile
+                    else:
+                        acc[slot] += tile
             return 0
 
-        lax.fori_loop(first, last, one, 0)
+        lax.fori_loop(first // TOGETHER, last // TOGETHER, one, 0)
 
     def pass_on(j):
         across[j].wait_recv()
@@ -172,16 +182,13 @@
     spread(0, range(blocks))
     fill.wait()
     all_groups = acc.shape[0] // GROUP
-    multiply(0, range(blocks), 0, all_groups // 2)
-    forward = [pass_on(0)]
-    multiply(0, range(blocks), all_groups // 2, all_groups)
-    for j in range(blocks):
-        for copy in forward[j]:
+    multiply(0, range(blocks), 0, all_groups)
+    forward = [pass_on(j) for j in range(blocks)]
+    for made in forward:
+        for copy in made:
             copy.wait_recv()
-        spread(1, [j])
-        multiply(1, [j], 0, all_groups)
-        if j + 1 < blocks:
-            forward.append(pass_on(j + 1))
+    spread(1, range(blocks))
+    multiply(1, range(blocks), 0, all_groups)
     forward = [copy for made in forward for copy in made]
 
     per_block = NXC * CAP
@@ -220,7 +227,7 @@
             at = pl.multiple_of(((y + d) % NY) * 16, 16)
             for g in range(groups):
                 values = jnp.concatenate(
-                    [acc[index_ref[first + g * 8 + n], pl.ds(at, 16), :][None] for n in range(8)], axis=0
+                    [acc[plan_ref[blocks * fits, first + g * 8 + n], pl.ds(at, 16), :][None] for n in range(8)], axis=0
                 )
                 whole, scale = coded(values)
                 qy[i, d - 1, g * 8 : g * 8 + 8] = whole
@@ -240,7 +247,7 @@
             halves = ([], [])
             for rank in range(CAP):
                 n = other * CAP + rank
-                tile = acc[index_ref[first + n], pl.ds(mine, 16), :]
+                tile = acc[plan_ref[blocks * fits, first + n], pl.ds(mine, 16), :]
                 for d in range(NY - 1):
                     tile = tile + decoded(ry[i, d, n]) * rsy[i, d, n // 8]
                 a, b = tile[:8], tile[8:]
@@ -379,17 +386,17 @@
     lax.fori_loop(1, NZL, sent_a, 0)
 
 
-def exchange(table, occ_of, index, occ, rows, target):
+def exchange(plan, occ, rows, target):
     i16, f32, bf16 = jnp.int16, jnp.float32, jnp.bfloat16
     blocks, occs = occ.shape[0] // FB, occ.shape[1] // OB
     fits = NY * NZH
-    slots = table.shape[1]
+    slots = TILES + occs * GROUP
     dma = pltpu.SemaphoreType.DMA
     smem, vmem = pl.BlockSpec(memory_space=pltpu.SMEM), pl.BlockSpec(memory_space=pltpu.VMEM)
     return pl.pallas_call(
         exchange_kernel,
         out_shape=jax.ShapeDtypeStruct((OWN_CAP, AB // fits, occ.shape[1]), bf16),
-        in_specs=[smem, smem, smem, vmem, pl.BlockSpec(memory_space=pl.ANY), vmem],
+        in_specs=[smem, vmem, pl.BlockSpec(memory_space=pl.ANY), vmem],
         out_specs=vmem,
         scratch_shapes=[
             pltpu.VMEM((fits,) + occ.shape, bf16),
@@ -417,84 +424,127 @@
         ],
         compiler_params=pltpu.CompilerParams(collective_id=0, has_side_effects=True, vmem_limit_bytes=48 << 20),
         name="exchange",
-    )(table, occ_of, index, occ, rows, target)
-
-
-def before(n):
-    at = jnp.arange(n)
-    return (at[:, None] < at[None, :]).astype(jnp.float32)
-
-
-def earlier_like(values):
-    at = jnp.arange(values.shape[0])
-    same = (values[:, None] == values[None, :]) & (at[None, :] < at[:, None])
-    return jnp.sum(same.astype(jnp.int32), axis=1)
-
-
-def plan(codes, occs, tiles_slots):
-    occ_of = codes % occs
-    kinds = jnp.arange(occs)
-    counts = jnp.sum((occ_of[None, :] == kinds[:, None]).astype(jnp.int32), axis=1)
-    padded = (counts + GROUP - 1) // GROUP * GROUP
-    starts = jnp.sum(jnp.where(kinds[None, :] < kinds[:, None], padded[None, :], 0), axis=1)
-    slot = earlier_like(occ_of) + jnp.sum(jnp.where(occ_of[:, None] == kinds[None, :], starts[None, :], 0), axis=1)
-    firsts = jnp.arange(tiles_slots // GROUP) * GROUP
-    group_occ = jnp.sum((firsts[:, None] >= starts[None, :]).astype(jnp.int32), axis=1) - 1
-    return slot, group_occ
-
-
-def pair_table(row_tiles, row_pairs, live_rows, slot, slots, none):
-    blocks, steps, width = row_pairs.shape
-    per_step = none // steps
-    usable = (row_pairs >= 0) & (jnp.arange(width) < live_rows[:, None])[None]
-    at = jnp.sum(jnp.where(row_tiles[:, :, None] == jnp.arange(slot.shape[0]), slot, 0), axis=2)
-    value = jnp.where(usable, row_pairs + (jnp.arange(steps) * per_step)[None, :, None] - none, 0)
-    hit = at[None, :, None, :] == jnp.arange(slots)[None, None, :, None]
-    return (jnp.sum(jnp.where(hit, value[:, :, None, :], 0), axis=3) + none).reshape(blocks * steps, slots)
-
-
-def routing(tile_list, codes, owner_slot, slot, column, occs):
-    blocks = owner_slot.shape[0]
-    tiles = codes.shape[0]
-    ao_count = tile_list.shape[0]
-    numbers = jnp.arange(blocks)
-    owned_at = jnp.sum(jnp.where((codes // occs)[:, None] == numbers, owner_slot, 0), axis=1)
-    owners = owned_at // OWN_CAP
-    places = owners * CAP + earlier_like(owners)
-    index = jnp.sum(jnp.where(places[None, :] == jnp.arange(ao_count * CAP)[:, None], slot[None, :], 0), axis=1)
-
-    mine = column * OWN_CAP + jnp.arange(OWN_CAP)
-    held = jnp.sum(jnp.where(owner_slot[None, :] == mine[:, None], numbers[None, :] + 1, 0), axis=1) - 1
-    names = tile_list // occs
-    place = jnp.sum(
-        jnp.where(names[:, :, None] == held[None, None, :], jnp.arange(OWN_CAP) + 1, 0), axis=2
-    ) - 1
-    owned = place >= 0
-    goal = (tile_list % occs) * OWN_CAP + place
-    rank = jnp.dot(owned.astype(jnp.float32), before(tiles)).astype(jnp.int32)
-    target = jnp.stack(
-        [jnp.sum(jnp.where(owned & (rank == r), goal + 1, 0), axis=1) - 1 for r in range(CAP)], axis=1
-    )
-    target = target.reshape(NZL, NXC, CAP)
-    sources = (column // NXC - offset(jnp.arange(NZL))) % NZL
-    turned = jnp.sum(
-        jnp.where((sources[:, None] == jnp.arange(NZL)[None, :])[:, :, None, None], target[None], 0), axis=1
-    )
-    turned = turned.reshape(PARTS, NZL // PARTS, NXC, CAP).transpose(0, 2, 1, 3)
-    turned = jnp.broadcast_to(turned[:, :, :, None], (PARTS, NXC, NZL // PARTS, NZH, CAP))
-    return index, turned.reshape(PARTS, -1)
+    )(plan, occ, rows, target)
+
+
+def prepare_kernel(tiles_ref, pairs_ref, live_ref, list_ref, owner_ref, plan_ref, target_ref):
+    f32, bf16 = jnp.float32, jnp.bfloat16
+    ao = lax.axis_index("ao")
+    zl = ao // NXC
+    fits, width = tiles_ref.shape
+    blocks = pairs_ref.shape[0]
+    columns, tiles = list_ref.shape
+    aos = owner_ref.shape[1]
+    occs = OCCS
+    slots = plan_ref.shape[1]
+    none = fits * PAIRS
+
+    def at(shape, axis):
+        return lax.broadcasted_iota(jnp.int32, shape, axis)
+
+    def dot(a, b):
+        return jnp.dot(a.astype(bf16), b.astype(bf16), preferred_element_type=f32)
+
+    def flip(a):
+        n = a.shape[1]
+        eye = (at((n, n), 0) == at((n, n), 1)).astype(bf16)
+        return lax.dot_general(eye, a.astype(bf16), (((1,), (1,)), ((), ())), preferred_element_type=f32)
+
+    def total(mask, value, axis):
+        return jnp.sum(jnp.where(mask, value, 0.0), axis=axis, keepdims=True)
+
+    codes = list_ref[pl.ds(ao, 1), :]
+    eight = at((8, tiles), 0)
+    both = jnp.where(eight == 0, codes & (occs - 1), codes >> OCC_BITS)
+    turned = flip(both.astype(f32))
+    occ_l = (codes & (occs - 1)).astype(f32)
+    occ_s, block_s = turned[:, 0:1], turned[:, 1:2]
+    row, lane = at((tiles, tiles), 0), at((tiles, tiles), 1)
+    slot_l = total((occ_s == occ_l) & (row < lane), 1.0, 0)
+    start = jnp.zeros((1, 1), f32)
+    groups = at((1, slots), 1) * GROUP
+    group_occ = jnp.zeros((1, slots), f32)
+    for o in range(occs):
+        slot_l = slot_l + jnp.where(occ_l == o, start, 0.0)
+        if o:
+            group_occ = group_occ + jnp.where(groups.astype(f32) >= start, 1.0, 0.0)
+        count = total(occ_l == o, 1.0, 1)
+        start = start + jnp.floor((count + (GROUP - 1)) * (1.0 / GROUP)) * GROUP
+
+    owner_row = owner_ref[...].astype(f32)
+    where_s = total(block_s == at((tiles, aos), 1).astype(f32), owner_row, 1)
+    owner_s = jnp.floor(where_s * (1.0 / OWN_CAP))
+    eye = row == lane
+    owner_l = total(eye, owner_s, 0)
+    slot_s = total(eye, slot_l, 1)
+    place_l = owner_l * CAP + total((owner_s == owner_l) & (row < lane), 1.0, 0)
+    place_s = total(eye, place_l, 1)
+    wide = at((tiles, slots), 1).astype(f32)
+    index = total(place_s == wide, slot_s, 0)
+
+    live_s = total(at((fits, fits), 0) == at((fits, fits), 1), live_ref[...].astype(f32), 1)
+    inside = at((fits, width), 1).astype(f32) < live_s
+    values = []
+    for j in range(blocks):
+        pair = pairs_ref[j]
+        value = (pair + at((fits, width), 0) * PAIRS - none).astype(f32)
+        values.append(jnp.where((pair.astype(f32) >= 0.0) & inside, value, 0.0))
+    values = jnp.concatenate(values, axis=0)
+    rows_s = flip(tiles_ref[...].astype(f32))
+    step_of = at(values.shape, 0) % fits
+    by_tile = jnp.zeros((values.shape[0], tiles), f32)
+    for s in range(fits):
+        hit = (rows_s[:, s : s + 1] == at((width, tiles), 1).astype(f32)).astype(f32)
+        by_tile = by_tile + jnp.where(step_of == s, dot(values, hit), 0.0)
+    table = dot(by_tile, (slot_s == wide).astype(f32)) + none
+    high = values.shape[0]
+    plan_ref[0:high, :] = table.astype(jnp.int32)
+    last = at((8, slots), 0)
+    extra = jnp.where(last == 0, index, jnp.where(last == 1, group_occ, 0.0))
+    plan_ref[high : high + 8, :] = extra.astype(jnp.int32)
+
+    mine = (ao * OWN_CAP + at((OWN_CAP, aos), 0)).astype(f32)
+    held = total(owner_row == mine, (at((OWN_CAP, aos), 1) + 1).astype(f32), 1) - 1.0
+    listed = list_ref[...]
+    names = (listed >> OCC_BITS).astype(f32)
+    place = jnp.full(names.shape, -1.0, f32)
+    for i in range(OWN_CAP):
+        place = jnp.where(names == held[i : i + 1, :], float(i), place)
+    owned = place >= 0.0
+    goal = (listed & (occs - 1)).astype(f32) * OWN_CAP + place
+    rank = dot(jnp.where(owned, 1.0, 0.0), (row < lane).astype(f32))
+    goals = [total(owned & (rank == r), goal + 1.0, 1) for r in range(CAP)]
+    span = NZL // PARTS
+    entry = at((columns, target_ref.shape[1]), 1)
+    column = at((columns, target_ref.shape[1]), 0)
+    rank_of, turn = entry % CAP, entry // (CAP * NZH) % span
+    side = entry // (CAP * NZH * span)
+    for part in range(PARTS):
+        k = part * span + turn
+        source = (zl - offset(k) + NZL) % NZL * NXC + side
+        goal_of = jnp.where(rank_of == 0, goals[0], goals[1])
+        target_ref[part : part + 1, :] = (total(column == source, goal_of, 0) - 1.0).astype(jnp.int32)
+
+
+def prepare(row_tiles, row_pairs, live_rows, tile_list, owner_slot):
+    blocks, fits, width = row_pairs.shape
+    vmem = pl.BlockSpec(memory_space=pltpu.VMEM)
+    return pl.pallas_call(
+        prepare_kernel,
+        out_shape=[
+            jax.ShapeDtypeStruct((blocks * fits + 8, 128), jnp.int32),
+            jax.ShapeDtypeStruct((PARTS, NXC * NZL // PARTS * NZH * CAP), jnp.int32),
+        ],
+        in_specs=[vmem] * 5,
+        out_specs=[vmem] * 2,
+        name="prepare",
+    )(row_tiles, row_pairs, live_rows, tile_list, owner_slot.reshape(1, -1))
 
 
 def shards(occ_blocks, resident, row_tiles, row_pairs, live_rows, tile_list, owner_slot):
-    column = lax.axis_index("ao")
-    occs = occ_blocks.shape[1] // OB
-    codes = lax.dynamic_index_in_dim(tile_list, column, 0, keepdims=False)
-    slots = codes.shape[0] + occs * GROUP
-    slot, group_occ = plan(codes, occs, slots)
-    table = pair_table(row_tiles[0], row_pairs[:, 0], live_rows[0], slot, slots, resident.shape[0])
-    index, target = routing(tile_list, codes, owner_slot, slot, column, occs)
+    plan, target = prepare(row_tiles[0], row_pairs[:, 0], live_rows, tile_list, owner_slot)
     rows = resident.reshape(resident.shape[0], AB // 2, 2 * FB)
-    return exchange(table, group_occ, index, occ_blocks, rows, target)
+    return exchange(plan, occ_blocks, rows, target)
 
 
 def solution(mesh):

time: 117 us -> 93 us (0.79)
  Pallas kernels: 104 us -> 89.5 us
  other arithmetic: 8.43 us -> 0 us
    pallas_call x1, Pallas kernels: 104 us -> 87.4 us  [exchange(): pl.pallas_call(exchange_kernel, out_shape=jax.ShapeDtypeStruct((OWN_CAP,...]
    reduce_sum x13 -> x0, other arithmetic: 4.37 us -> none  [the longest x1 1.04 us: pair_table(): jnp.sum(jnp.where(row_tiles[:, :, None] == jnp.arange(slot.shape[0]), slo...]
    select_n x6 -> x0, other arithmetic: 2.3 us -> none  [the longest x1 0.78 us: pair_table(): jnp.where(usable, row_pairs + (jnp.arange(steps) * per_step)[None, :, Non...]
    pallas_call x0 -> x1, Pallas kernels: none -> 2.06 us  [prepare(): pl.pallas_call(prepare_kernel, out_shape=[jax.ShapeDtypeStruct((blocks *...]
    unnamed x4 -> x8, local copies, waits for them, and re-layouts: 2.75 us -> 2.75 us
where the time goes in v4:
time: 93 us; the launch traced here: 92.3 us
  Pallas kernels  89.5 us (96%)
  local copies, waits for them, and re-layouts  2.75 us (3%)
    pallas_call x1, Pallas kernels, exchange(): pl.pallas_call(exchange_kernel, out_shape=jax.ShapeDtypeStruct((OWN_CAP,...  87.4 us
    unnamed x8, local copies, waits for them, and re-layouts  2.75 us
    pallas_call x1, Pallas kernels, prepare(): pl.pallas_call(prepare_kernel, out_shape=[jax.ShapeDtypeStruct((blocks *...  2.06 us

profile of v4, /device:TPU:1, one launch (start us, length us, event | category | flops | bytes accessed | tf_op | source)
XLA Modules:
  0.0 92.3 jit_solution(8671174756429920257)
XLA Ops:
  0.0 2.1 %prepare.1 = (s32[32,128]{1,0:T(8,128)}, s32[4,64]{1,0:T(4,128)}) custom-call(s32[8,96]{1,0:T(8,128)} %bitcast.8, s32[3,8,96]{2,1,0:T(8,128)} %bitcast.7, s32[1,8]{1,0:T(1,128)} %live_ref.1, s32[64,96]{1,0:T(8,128)} %list_ref.1, s32[1,256]{1,0:T(1,128)} %bitcast.9), custom_call_target="tpu_custom_call" | custom-call | tf_op jit(solution)/shard_map/prepare/pallas_call | solution.py:532
  2.1 0.0 copy-start
  2.1 0.0 copy-start.1
  2.1 0.0 copy-start.2
  2.1 2.1 %copy.8 = bf16[32,8,32,128]{3,2,1,0:T(8,128)(2,1)S(1)} copy(bf16[32,8,32,128]{3,1,2,0:T(8,128)(2,1)} %bitcast.6) | data formatting | bytes 4194304
  4.2 0.0 copy-done
  4.2 0.0 copy-done.1
  4.2 0.0 copy-done.2
  4.2 87.4 %exchange.1 = bf16[8,8,512]{2,1,0:T(8,128)(2,1)S(1)} custom-call(s32[32,128]{1,0:T(8,128)S(1)} %copy-done.1, bf16[192,512]{1,0:T(8,128)(2,1)S(1)} %copy-done, bf16[256,32,128]{2,1,0:T(8,128)(2,1)S(1)} %bitcast.5, s32[4,64]{1,0:T(4,128)S(1)} %copy-done.2), custom_call_target="tpu_custom_call" | custom-call | tf_op jit(solution)/shard_map/exchange/pallas_call | solution.py:396
  91.6 0.6 copy.10
Async XLA Ops:
  2.1 2.1 %copy-start = (bf16[192,512]{1,0:T(8,128)(2,1)S(1)}, bf16[192,512]{1,0:T(8,128)(2,1)}, u32[]{:S(2)}) copy-start(bf16[192,512]{1,0:T(8,128)(2,1)} %x_ref.1) | copy-start | bytes 589828
  2.1 2.1 %copy-start.1 = (s32[32,128]{1,0:T(8,128)S(1)}, s32[32,128]{1,0:T(8,128)}, u32[]{:S(2)}) copy-start(s32[32,128]{1,0:T(8,128)} %get-tuple-element.7.plan_ref) | copy-start | bytes 49156
  2.1 2.1 %copy-start.2 = (s32[4,64]{1,0:T(4,128)S(1)}, s32[4,64]{1,0:T(4,128)}, u32[]{:S(2)}) copy-start(s32[4,64]{1,0:T(4,128)} %get-tuple-element.8.target_ref) | copy-start | bytes 3076

commit v5 on v4

--- a/solution.py
+++ b/solution.py
@@ -18,7 +18,7 @@
 NXC = 8
 GROUP = 4
 PARTS = 4
-TOGETHER = 4
+TOGETHER = 7
 TILES = 96
 OCCS = 4
 OCC_BITS = 2
@@ -44,9 +44,9 @@
 
 
 def exchange_kernel(
-    plan_ref, x_ref, res_ref, target_ref, out_ref,
-    occ_all, wide, res, acc, qy, sy, ry, rsy, qa, sa, ra, rsa, rb, rsb, flat, summed, final,
-    send_own, recv_own, send_z, recv_z, send_fw, recv_fw, local_sem,
+    plan_in, x_ref, res_ref, target_in, out_ref,
+    plan_ref, target_ref, occ_all, wide, raw, res, acc, qy, sy, ry, rsy, qa, sa, ra, rsa, rb, rsb, flat, summed, final,
+    send_own, recv_own, send_z, recv_z, send_fw, recv_fw, local_sem, plan_sem, target_sem, own_sem,
     send_y, recv_y, send_a, recv_a, send_b, recv_b,
 ):
     fit = lax.axis_index("fit")
@@ -70,8 +70,14 @@
     def at_x(d):
         return (fit, zl * NXC + (xc + d) % NXC)
 
-    fill = pltpu.make_async_copy(res_ref, res.at[pl.ds(0, tiles)], local_sem)
+    fill = pltpu.make_async_copy(res_ref, raw, local_sem)
     fill.start()
+    plan_copy = pltpu.make_async_copy(plan_in, plan_ref, plan_sem)
+    plan_copy.start()
+    target_copy = pltpu.make_async_copy(target_in, target_ref, target_sem)
+    target_copy.start()
+    own_copy = pltpu.make_async_copy(x_ref, occ_all.at[fit], own_sem)
+    own_copy.start()
     barrier = pltpu.get_barrier_semaphore()
     pl.semaphore_signal(barrier, inc=1, device_id=(partner, ao), device_id_type=MESH)
     for d in range(1, NY):
@@ -110,7 +116,15 @@
 
     wide[...] = jnp.zeros_like(wide)
     res[tiles] = jnp.zeros(res.shape[1:], res.dtype)
-    occ_all[fit] = x_ref[...]
+    fill.wait()
+
+    def lay(s, _):
+        at = pl.multiple_of(s * 16, 16)
+        pieces = [raw[pl.ds(at, 16), m * OB : (m + 1) * OB] for m in range(AB // 2)]
+        res[pl.ds(at, 16)] = jnp.swapaxes(jnp.stack(pieces, axis=0), 0, 1)
+        return 0
+
+    lax.fori_loop(0, tiles // 16, lay, 0)
 
     def place(part, i, j):
         return (i * blocks + j if part == 0 else (fits // 2) * (blocks + j) + i) * 2 * FB
@@ -179,15 +193,20 @@
 
     for copy in own:
         copy.wait_recv()
+    own_copy.wait()
     spread(0, range(blocks))
-    fill.wait()
+    plan_copy.wait()
+    target_copy.wait()
     all_groups = acc.shape[0] // GROUP
     multiply(0, range(blocks), 0, all_groups)
-    forward = [pass_on(j) for j in range(blocks)]
-    for made in forward:
-        for copy in made:
-            copy.wait_recv()
-    spread(1, range(blocks))
+    forward = []
+    for j in range(blocks + 1):
+        if j < blocks:
+            forward.append(pass_on(j))
+        if j:
+            for copy in forward[j - 1]:
+                copy.wait_recv()
+            spread(1, [j - 1])
     multiply(1, range(blocks), 0, all_groups)
     forward = [copy for made in forward for copy in made]
 
@@ -265,8 +284,11 @@
             for copy in copies_a(i, other):
                 copy.start()
 
-    code(0)
-    code(1)
+    def code_one(i, _):
+        code(i)
+        return 0
+
+    lax.fori_loop(0, NZL, code_one, 0)
     collect(0)
     first_a = copies_a(0, 1 - zh)
     for copy in first_a:
@@ -275,7 +297,6 @@
     rsa[0, zh] = sa[0, zh]
 
     def turn(i, _):
-        code(i + 1)
         collect(i)
         send_on(i)
         return 0
@@ -392,16 +413,19 @@
     fits = NY * NZH
     slots = TILES + occs * GROUP
     dma = pltpu.SemaphoreType.DMA
-    smem, vmem = pl.BlockSpec(memory_space=pltpu.SMEM), pl.BlockSpec(memory_space=pltpu.VMEM)
+    vmem = pl.BlockSpec(memory_space=pltpu.VMEM)
     return pl.pallas_call(
         exchange_kernel,
         out_shape=jax.ShapeDtypeStruct((OWN_CAP, AB // fits, occ.shape[1]), bf16),
-        in_specs=[smem, vmem, pl.BlockSpec(memory_space=pl.ANY), vmem],
+        in_specs=[pl.BlockSpec(memory_space=pltpu.HBM)] * 4,
         out_specs=vmem,
         scratch_shapes=[
+            pltpu.SMEM(plan.shape, jnp.int32),
+            pltpu.VMEM(target.shape, jnp.int32),
             pltpu.VMEM((fits,) + occ.shape, bf16),
             pltpu.VMEM((occs, fits * blocks * 2 * FB, 2 * OB), bf16),
-            pltpu.VMEM((rows.shape[0] + 1,) + rows.shape[1:], bf16),
+            pltpu.VMEM(rows.shape, bf16),
+            pltpu.VMEM((rows.shape[0] + 1, AB // 2, 2 * FB), bf16),
             pltpu.VMEM((slots, AB, OB), f32),
             pltpu.VMEM((NZL, NY - 1, NXC * CAP, 16, OB), i16),
             pltpu.VMEM((NZL, NY - 1, NXC * CAP // 8, 1, OB), f32),
@@ -417,12 +441,12 @@
             pltpu.VMEM((8, occs * OWN_CAP, OB), f32),
             pltpu.VMEM((occs, OWN_CAP * 8, OB), f32),
             dma((NY - 1,)), dma((NY - 1,)), dma((blocks,)), dma((blocks,)),
-            dma((blocks, NY - 1)), dma((blocks, NY - 1)), dma,
+            dma((blocks, NY - 1)), dma((blocks, NY - 1)), dma, dma, dma, dma,
             dma((NZL, 2, NY - 1)), dma((NZL, 2, NY - 1)),
             dma((NZL, 2, NZH)), dma((NZL, 2, NZH)),
             dma((PARTS, 2, NXC - 1)), dma((PARTS, 2, NXC - 1)),
         ],
-        compiler_params=pltpu.CompilerParams(collective_id=0, has_side_effects=True, vmem_limit_bytes=48 << 20),
+        compiler_params=pltpu.CompilerParams(collective_id=0, has_side_effects=True, vmem_limit_bytes=58 << 20),
         name="exchange",
     )(plan, occ, rows, target)
 
@@ -543,8 +567,7 @@
 
 def shards(occ_blocks, resident, row_tiles, row_pairs, live_rows, tile_list, owner_slot):
     plan, target = prepare(row_tiles[0], row_pairs[:, 0], live_rows, tile_list, owner_slot)
-    rows = resident.reshape(resident.shape[0], AB // 2, 2 * FB)
-    return exchange(plan, occ_blocks, rows, target)
+    return exchange(plan, occ_blocks, resident, target)
 
 
 def solution(mesh):

time: 93 us -> 90 us (0.968)
  local copies, waits for them, and re-layouts: 2.75 us -> 1.47 us
  Pallas kernels: 89.5 us -> 88.3 us
    unnamed x8 -> x1, local copies, waits for them, and re-layouts: 2.75 us -> 1.47 us
    pallas_call x1, Pallas kernels: 87.4 us -> 86.3 us  [exchange(): pl.pallas_call(exchange_kernel, out_shape=jax.ShapeDtypeStruct((OWN_CAP,...]
where the time goes in v5:
time: 90 us; the launch traced here: 89.8 us
  Pallas kernels  88.3 us (98%)
  local copies, waits for them, and re-layouts  1.47 us (2%)
    pallas_call x1, Pallas kernels, exchange(): pl.pallas_call(exchange_kernel, out_shape=jax.ShapeDtypeStruct((OWN_CAP,...  86.3 us
    pallas_call x1, Pallas kernels, prepare(): pl.pallas_call(prepare_kernel, out_shape=[jax.ShapeDtypeStruct((blocks *...  2.06 us

profile of v5, /device:TPU:1, one launch (start us, length us, event | category | flops | bytes accessed | tf_op | source)
XLA Modules:
  0.0 89.8 jit_solution(852551221341884541)
XLA Ops:
  0.0 2.1 %prepare.1 = (s32[32,128]{1,0:T(8,128)}, s32[4,64]{1,0:T(4,128)}) custom-call(s32[8,96]{1,0:T(8,128)} %bitcast.4, s32[3,8,96]{2,1,0:T(8,128)} %bitcast.3, s32[1,8]{1,0:T(1,128)} %live_ref.1, s32[64,96]{1,0:T(8,128)} %list_ref.1, s32[1,256]{1,0:T(1,128)} %bitcast.5), custom_call_target="tpu_custom_call" | custom-call | tf_op jit(solution)/shard_map/prepare/pallas_call | solution.py:556
  2.1 86.3 %exchange.1 = bf16[8,8,512]{2,1,0:T(8,128)(2,1)} custom-call(s32[32,128]{1,0:T(8,128)} %get-tuple-element.7.plan_in, bf16[192,512]{1,0:T(8,128)(2,1)} %x_ref.1, bf16[256,4096]{1,0:T(8,128)(2,1)} %res_ref.1, s32[4,64]{1,0:T(4,128)} %get-tuple-element.8.target_in), custom_call_target="tpu_custom_call" | custom-call | tf_op jit(solution)/shard_map/exchange/pallas_call | solution.py:417
  88.3 1.5 %copy.9 = bf16[8,8,512]{2,1,0:T(8,128)(2,1)} copy(bf16[8,8,512]{2,1,0:T(8,128)(2,1)} %exchange.1) | data formatting | bytes 131072

commit v6 on v5

--- a/solution.py
+++ b/solution.py
@@ -44,9 +44,9 @@
 
 
 def exchange_kernel(
-    plan_in, x_ref, res_ref, target_in, out_ref,
-    plan_ref, target_ref, occ_all, wide, raw, res, acc, qy, sy, ry, rsy, qa, sa, ra, rsa, rb, rsb, flat, summed, final,
-    send_own, recv_own, send_z, recv_z, send_fw, recv_fw, local_sem, plan_sem, target_sem, own_sem,
+    tiles_in, pairs_in, live_in, list_in, owner_in, x_ref, res_ref, out_ref,
+    tiles_ref, pairs_ref, live_ref, list_ref, owner_ref, plan_made, plan_ref, target_ref, occ_all, wide, raw, res, acc, qy, sy, ry, rsy, qa, sa, ra, rsa, rb, rsb, flat, summed, final,
+    send_own, recv_own, send_z, recv_z, send_fw, recv_fw, local_sem, plan_sem, table_sem, own_sem,
     send_y, recv_y, send_a, recv_a, send_b, recv_b,
 ):
     fit = lax.axis_index("fit")
@@ -72,10 +72,10 @@
 
     fill = pltpu.make_async_copy(res_ref, raw, local_sem)
     fill.start()
-    plan_copy = pltpu.make_async_copy(plan_in, plan_ref, plan_sem)
-    plan_copy.start()
-    target_copy = pltpu.make_async_copy(target_in, target_ref, target_sem)
-    target_copy.start()
+    pairs = ((tiles_in, tiles_ref), (pairs_in, pairs_ref), (live_in, live_ref), (list_in, list_ref), (owner_in, owner_ref))
+    tables = [pltpu.make_async_copy(src, dst, table_sem.at[n]) for n, (src, dst) in enumerate(pairs)]
+    for copy in tables:
+        copy.start()
     own_copy = pltpu.make_async_copy(x_ref, occ_all.at[fit], own_sem)
     own_copy.start()
     barrier = pltpu.get_barrier_semaphore()
@@ -191,12 +191,16 @@
             made.append(copy)
         return made
 
+    for copy in tables:
+        copy.wait()
+    prepare_plan(tiles_ref, pairs_ref, live_ref, list_ref, owner_ref, plan_made, target_ref)
+    plan_copy = pltpu.make_async_copy(plan_made, plan_ref, plan_sem)
+    plan_copy.start()
     for copy in own:
         copy.wait_recv()
     own_copy.wait()
     spread(0, range(blocks))
     plan_copy.wait()
-    target_copy.wait()
     all_groups = acc.shape[0] // GROUP
     multiply(0, range(blocks), 0, all_groups)
     forward = []
@@ -407,21 +411,24 @@
     lax.fori_loop(1, NZL, sent_a, 0)
 
 
-def exchange(plan, occ, rows, target):
+def exchange(row_tiles, row_pairs, live_rows, tile_list, owner_slot, occ, rows):
     i16, f32, bf16 = jnp.int16, jnp.float32, jnp.bfloat16
     blocks, occs = occ.shape[0] // FB, occ.shape[1] // OB
     fits = NY * NZH
     slots = TILES + occs * GROUP
+    tables = (row_tiles, row_pairs, live_rows, tile_list, owner_slot.reshape(1, -1))
     dma = pltpu.SemaphoreType.DMA
     vmem = pl.BlockSpec(memory_space=pltpu.VMEM)
     return pl.pallas_call(
         exchange_kernel,
         out_shape=jax.ShapeDtypeStruct((OWN_CAP, AB // fits, occ.shape[1]), bf16),
-        in_specs=[pl.BlockSpec(memory_space=pltpu.HBM)] * 4,
+        in_specs=[pl.BlockSpec(memory_space=pltpu.HBM)] * 7,
         out_specs=vmem,
         scratch_shapes=[
-            pltpu.SMEM(plan.shape, jnp.int32),
-            pltpu.VMEM(target.shape, jnp.int32),
+            *[pltpu.VMEM(table.shape, jnp.int32) for table in tables],
+            pltpu.VMEM((blocks * fits + 8, 128), jnp.int32),
+            pltpu.SMEM((blocks * fits + 8, 128), jnp.int32),
+            pltpu.VMEM((PARTS, NXC * NZL // PARTS * NZH * CAP), jnp.int32),
             pltpu.VMEM((fits,) + occ.shape, bf16),
             pltpu.VMEM((occs, fits * blocks * 2 * FB, 2 * OB), bf16),
             pltpu.VMEM(rows.shape, bf16),
@@ -441,17 +448,17 @@
             pltpu.VMEM((8, occs * OWN_CAP, OB), f32),
             pltpu.VMEM((occs, OWN_CAP * 8, OB), f32),
             dma((NY - 1,)), dma((NY - 1,)), dma((blocks,)), dma((blocks,)),
-            dma((blocks, NY - 1)), dma((blocks, NY - 1)), dma, dma, dma, dma,
+            dma((blocks, NY - 1)), dma((blocks, NY - 1)), dma, dma, dma((5,)), dma,
             dma((NZL, 2, NY - 1)), dma((NZL, 2, NY - 1)),
             dma((NZL, 2, NZH)), dma((NZL, 2, NZH)),
             dma((PARTS, 2, NXC - 1)), dma((PARTS, 2, NXC - 1)),
         ],
         compiler_params=pltpu.CompilerParams(collective_id=0, has_side_effects=True, vmem_limit_bytes=58 << 20),
         name="exchange",
-    )(plan, occ, rows, target)
-
-
-def prepare_kernel(tiles_ref, pairs_ref, live_ref, list_ref, owner_ref, plan_ref, target_ref):
+    )(*tables, occ, rows)
+
+
+def prepare_plan(tiles_ref, pairs_ref, live_ref, list_ref, owner_ref, plan_ref, target_ref):
     f32, bf16 = jnp.float32, jnp.bfloat16
     ao = lax.axis_index("ao")
     zl = ao // NXC
@@ -522,10 +529,11 @@
         by_tile = by_tile + jnp.where(step_of == s, dot(values, hit), 0.0)
     table = dot(by_tile, (slot_s == wide).astype(f32)) + none
     high = values.shape[0]
-    plan_ref[0:high, :] = table.astype(jnp.int32)
+    plan_ref[0:high, :] = jnp.clip(table.astype(jnp.int32), 0, none)
     last = at((8, slots), 0)
     extra = jnp.where(last == 0, index, jnp.where(last == 1, group_occ, 0.0))
-    plan_ref[high : high + 8, :] = extra.astype(jnp.int32)
+    most = jnp.where(last == 0, TILES + occs * GROUP - 1, occs - 1)
+    plan_ref[high : high + 8, :] = jnp.minimum(jnp.maximum(extra.astype(jnp.int32), 0), most)
 
     mine = (ao * OWN_CAP + at((OWN_CAP, aos), 0)).astype(f32)
     held = total(owner_row == mine, (at((OWN_CAP, aos), 1) + 1).astype(f32), 1) - 1.0
@@ -550,24 +558,8 @@
         target_ref[part : part + 1, :] = (total(column == source, goal_of, 0) - 1.0).astype(jnp.int32)
 
 
-def prepare(row_tiles, row_pairs, live_rows, tile_list, owner_slot):
-    blocks, fits, width = row_pairs.shape
-    vmem = pl.BlockSpec(memory_space=pltpu.VMEM)
-    return pl.pallas_call(
-        prepare_kernel,
-        out_shape=[
-            jax.ShapeDtypeStruct((blocks * fits + 8, 128), jnp.int32),
-            jax.ShapeDtypeStruct((PARTS, NXC * NZL // PARTS * NZH * CAP), jnp.int32),
-        ],
-        in_specs=[vmem] * 5,
-        out_specs=[vmem] * 2,
-        name="prepare",
-    )(row_tiles, row_pairs, live_rows, tile_list, owner_slot.reshape(1, -1))
-
-
 def shards(occ_blocks, resident, row_tiles, row_pairs, live_rows, tile_list, owner_slot):
-    plan, target = prepare(row_tiles[0], row_pairs[:, 0], live_rows, tile_list, owner_slot)
-    return exchange(plan, occ_blocks, resident, target)
+    return exchange(row_tiles[0], row_pairs[:, 0], live_rows, tile_list, owner_slot, occ_blocks, resident)
 
 
 def solution(mesh):

time: 90 us -> 88 us (0.978)
  Pallas kernels: 88.3 us -> 86.3 us
    pallas_call x1 -> x0, Pallas kernels: 2.06 us -> none  [prepare(): pl.pallas_call(prepare_kernel, out_shape=[jax.ShapeDtypeStruct((blocks *...]
where the time goes in v6:
time: 88 us; the launch traced here: 87.8 us
  Pallas kernels  86.3 us (98%)
  local copies, waits for them, and re-layouts  1.47 us (2%)
    pallas_call x1, Pallas kernels, exchange(): pl.pallas_call(exchange_kernel, out_shape=jax.ShapeDtypeStruct((OWN_CAP,...  86.3 us

profile of v6, /device:TPU:1, one launch (start us, length us, event | category | flops | bytes accessed | tf_op | source)
XLA Modules:
  0.0 87.8 jit_solution(3112558130652552727)
XLA Ops:
  0.0 86.3 %exchange.1 = bf16[8,8,512]{2,1,0:T(8,128)(2,1)} custom-call(s32[8,96]{1,0:T(8,128)} %bitcast.4, s32[3,8,96]{2,1,0:T(8,128)} %bitcast.3, s32[1,8]{1,0:T(1,128)} %live_in.1, s32[64,96]{1,0:T(8,128)} %list_in.1, s32[1,256]{1,0:T(1,128)} %bitcast.5, bf16[192,512]{1,0:T(8,128)(2,1)} %x_ref.1, bf16[256,4096]{1,0:T(8,128)(2,1)} %res_ref.1), custom_call_target="tpu_custom_call" | custom-call | tf_op jit(solution)/shard_map/exchange/pallas_call | solution.py:422
  86.3 1.5 %copy.9 = bf16[8,8,512]{2,1,0:T(8,128)(2,1)} copy(bf16[8,8,512]{2,1,0:T(8,128)(2,1)} %exchange.1) | data formatting | bytes 131072
